TPU v7x, 256 devices: a whole 4x4x8 slice. The times are simulated.
256 devices in a mesh: seq: 64 (over y, z, core), head: 4 (over x).
Axes of the slice: x: 4, y: 4, z: 8, core: 2. Of those that a mesh axis runs over, the one named last changes fastest.
Arguments:
- tokens: bfloat16 [131072, 2048], P(('seq', 'head')), may hold values from -60 to 60
- query_index: int32 [8192], replicated, may hold values from 0 to 131071, as said below
- key_index: int32 [8192], replicated, may hold values from 0 to 131071, as said below
- light_query: bfloat16 [2048, 256], replicated, may hold values from -0.1875 to 0.1875
- light_key: bfloat16 [2048, 256], replicated, may hold values from -0.1875 to 0.1875
- light_value: bfloat16 [2048, 256], replicated, may hold values from -0.125 to 0.125
- light_out: bfloat16 [256, 2048], replicated, may hold values from -0.375 to 0.375
- heavy_query: bfloat16 [2048, 1024], P(None, 'head'), may hold values from -0.1875 to 0.1875
- heavy_key: bfloat16 [2048, 1024], P(None, 'head'), may hold values from -0.1875 to 0.1875
- heavy_value: bfloat16 [2048, 1024], P(None, 'head'), may hold values from -0.125 to 0.125
- heavy_out: bfloat16 [1024, 2048], P('head'), may hold values from -0.1875 to 0.1875
Outputs:
- layer_out: bfloat16 [131072, 2048], P(('seq', 'head'))
Inputs may be any that keep to these rules, and one draw needn't show every extreme that they name: `query_index`: ascending and distinct token positions; at most 512 of them lie in one block of 2048 tokens starting at a multiple of 2048, and some block holds exactly 512. `key_index`: ascending and distinct token positions; at most 192 of them lie in one block of 2048 tokens starting at a multiple of 2048, and some block holds exactly 192.
All inputs are finite; a program needn't handle non-finite values.
Results may differ from a plain program's by a relative error of at most 0.02.
Values may be sent and summed in bfloat16 or wider, within the bound.
No kernel may reach another device: no remote copies, remote signals or barrier semaphores. Data moves between devices by JAX's collectives and lax.ppermute only.
A program may use at most 128 MiB of HBM per device.

v0:
```python
import functools

import jax
import jax.numpy as jnp
from jax import lax
from jax.experimental import pallas as pl
from jax.experimental.pallas import tpu as pltpu
from jax.sharding import Mesh
from jax.sharding import PartitionSpec as P


HDIM = 64
RADIUS = 127
HALO = 128
ALL_AXES = ("y", "z", "c", "x")
LOW = -1e30
QTILE = 512
KCHUNK = 3072
Z_STEPS = (0, -1, 1, -2, 2, -3, 3, -4)


def shift(value, axis, distance):
    size = lax.axis_size(axis)
    return lax.ppermute(value, axis, [(i, (i + distance) % size) for i in range(size)])


def opposite(value):
    size = lax.axis_size("x")
    pairs = [(i, (i + 1) % size) for i in range(size)]
    pairs += [(size + i, size + (i - 1) % size) for i in range(size)]
    return lax.ppermute(value, ("c", "x"), pairs)


def gather_weights(shard):
    near = opposite(shard)
    half = shard.shape[0] // 2
    far = opposite(lax.dynamic_slice_in_dim(near, lax.axis_index("c") * half, half, 0))
    return (near, shift(near, "c", 1), far, shift(far, "c", 1))


def vmem():
    return pl.BlockSpec(memory_space=pltpu.VMEM)


def smem():
    return pl.BlockSpec(memory_space=pltpu.SMEM)


def cost(flops, moved, exps=0):
    return pl.CostEstimate(flops=flops, bytes_accessed=moved, transcendentals=exps)


def light_kernel(first_ref, q_ref, prev_ref, own_ref, next_ref, out_ref, padded, *, total):
    rows, width = q_ref.shape
    tile = 2 * HALO
    span = tile + 2 * HALO
    padded[:HALO] = prev_ref[...]
    padded[HALO : HALO + rows] = own_ref[...]
    padded[HALO + rows :] = next_ref[...]
    row = lax.broadcasted_iota(jnp.int32, (tile, span), 0)
    col = lax.broadcasted_iota(jnp.int32, (tile, span), 1)
    near = jnp.abs(col - HALO - row) <= RADIUS
    head_of = lax.broadcasted_iota(jnp.int32, (tile, width), 1) // HDIM

    def tile_step(number, unused):
        start = pl.multiple_of(number * tile, tile)
        position = first_ref[0] + start - HALO + col
        allowed = near & (position >= 0) & (position < total)
        q = q_ref[pl.ds(start, tile), :].astype(jnp.float32) * (HDIM**-0.5)
        keys = padded[pl.ds(start, span), :width]
        values = padded[pl.ds(start, span), width:]
        out = jnp.zeros((tile, width), jnp.float32)
        for head in range(width // HDIM):
            scores = lax.dot_general(
                jnp.where(head_of == head, q, 0.0).astype(jnp.bfloat16),
                keys,
                (((1,), (1,)), ((), ())),
                preferred_element_type=jnp.float32,
            )
            scores = jnp.where(allowed, scores, LOW)
            weights = jnp.exp(scores - jnp.max(scores, axis=1, keepdims=True))
            totals = jnp.sum(weights, axis=1, keepdims=True)
            mixed = jnp.dot(
                weights.astype(jnp.bfloat16), values, preferred_element_type=jnp.float32
            )
            out = jnp.where(head_of == head, mixed / totals, out)
        out_ref[pl.ds(start, tile), :] = out.astype(jnp.bfloat16)
        return unused

    lax.fori_loop(0, rows // tile, tile_step, 0)


def slot_list(index_ref, bound, cap):
    lines, lanes = index_ref.shape
    begin = jnp.sum(jnp.where(index_ref[...] < bound, 1.0, 0.0)).astype(jnp.int32)
    line = begin // lanes
    count = (cap + lanes - 1) // lanes + 1
    parts = []
    for step in range(count):
        values = index_ref[pl.ds(jnp.minimum(line + step, lines - 1), 1), :]
        parts.append(jnp.where(line + step < lines, values, -1))
    window = jnp.broadcast_to(jnp.concatenate(parts, axis=1), (8, count * lanes))
    size = count * lanes
    return pltpu.roll(window, (size - begin % lanes) % size, 1)[:1, :cap]


def hot_of(slots, rows):
    token = lax.broadcasted_iota(jnp.int32, (rows, slots.shape[1]), 0)
    return jnp.where(token == slots, 1.0, 0.0).astype(jnp.bfloat16)


def pick_rows(hot, rows):
    return lax.dot_general(
        hot, rows, (((0,), (0,)), ((), ())), preferred_element_type=jnp.float32
    ).astype(jnp.bfloat16)


def pick_kernel(place_ref, index_ref, tokens_ref, *refs):
    outs, picked = refs[:-1], refs[-1]
    groups = len(outs)
    quarter = outs[0].shape[0]
    rows = tokens_ref.shape[0]
    slots = slot_list(index_ref, place_ref[4], groups * quarter) - place_ref[5]
    picked[...] = pick_rows(hot_of(slots, rows), tokens_ref[...])
    for step in range(groups):
        group = (place_ref[3] + step) % groups
        outs[step][...] = picked[pl.ds(pl.multiple_of(group * quarter, 16), quarter), :]


def local_kernel(
    tokens_ref, query_ref, key_ref, value_ref, q_ref, pair_ref, head_ref, tail_ref
):
    rows = tokens_ref.shape[0]
    width = query_ref.shape[1]
    tile = rows // 2

    def tile_step(number, unused):
        span = pl.ds(pl.multiple_of(number * tile, tile), tile)
        tokens = tokens_ref[span, :]

        def times(weights):
            return jnp.dot(tokens, weights[...], preferred_element_type=jnp.float32).astype(
                jnp.bfloat16
            )

        q_ref[span, :] = times(query_ref)
        pair_ref[span, :width] = times(key_ref)
        pair_ref[span, width:] = times(value_ref)
        return unused

    lax.fori_loop(0, 2, tile_step, 0)
    head_ref[...] = pair_ref[:HALO]
    tail_ref[...] = pair_ref[rows - HALO :]


def project_kernel(
    place_ref, index_ref, tokens_ref, own_ref, near_ref, near2_ref, far_ref, far2_ref, *refs
):
    outs, slots_ref, far, dense = refs[:-3], refs[-3], refs[-2], refs[-1]
    core = place_ref[2]
    half = far_ref.shape[0]
    rows = tokens_ref.shape[0]
    tile = rows // 2
    far[pl.ds(pl.multiple_of(core * half, half), half), :] = far_ref[...]
    far[pl.ds(pl.multiple_of((1 - core) * half, half), half), :] = far2_ref[...]

    def tile_step(number, unused):
        span = pl.ds(pl.multiple_of(number * tile, tile), tile)
        tokens = tokens_ref[span, :]
        for group, weights in ((0, own_ref), (1 + core, near_ref), (2 - core, near2_ref), (3, far)):
            dense[group, span, :] = jnp.dot(
                tokens, weights[...], preferred_element_type=jnp.float32
            ).astype(jnp.bfloat16)
        return unused

    lax.fori_loop(0, 2, tile_step, 0)
    slots = slot_list(index_ref, place_ref[4], slots_ref.shape[1]) - place_ref[5]
    slots_ref[...] = slots
    hot = hot_of(slots, rows)
    for group, out in enumerate(outs):
        out[...] = pick_rows(hot, dense[group])


def pair_kernel(place_ref, own_ref, a_ref, b_ref, c_ref, key_ref, value_ref, out_ref, rows):
    quarter = own_ref.shape[0]
    for number, source in enumerate((own_ref, a_ref, b_ref, c_ref)):
        group = (place_ref[3] - number + 4) % 4
        rows[pl.ds(pl.multiple_of(group * quarter, 16), quarter), :] = source[...]
    every = rows[...]
    keys = jnp.dot(every, key_ref[...], preferred_element_type=jnp.float32).astype(jnp.bfloat16)
    values = jnp.dot(every, value_ref[...], preferred_element_type=jnp.float32).astype(
        jnp.bfloat16
    )
    size = 4 * quarter
    for head in range(out_ref.shape[0] // size):
        cols = slice(head * HDIM, (head + 1) * HDIM)
        out_ref[head * size : (head + 1) * size, :] = jnp.concatenate(
            [keys[:, cols], values[:, cols]], axis=1
        )


def query_kernel(own_ref, a_ref, b_ref, c_ref, out_ref):
    rows = own_ref[...] + a_ref[...] + b_ref[...] + c_ref[...]
    half = rows.shape[0] // 2
    for head in range(out_ref.shape[0] // half):
        cols = slice(head * HDIM, (head + 1) * HDIM)
        out_ref[head * half : (head + 1) * half, :] = jnp.concatenate(
            [rows[:half, cols], rows[half:, cols]], axis=1
        )


def exchange(value):
    return lax.all_to_all(value, "y", 0, 0, tiled=True)


def attention_kernel(place_ref, query_starts_ref, key_starts_ref, *refs, sizes):
    y_size, z_size = sizes
    q_ref, refs = refs[0], refs[1:]
    near_refs, refs = refs[:z_size], refs[z_size:]
    far_refs, refs = refs[:z_size], refs[z_size:]
    out_ref, queries, keys, values, results = refs
    pz, pc = place_ref[1], place_ref[2]
    half = q_ref.shape[0] // y_size
    key_cap = near_refs[0].shape[0] // y_size

    def block_of(by, step_z, swap):
        bz = (pz + step_z + z_size) % z_size
        bc = (pc + swap) % 2
        return (by * z_size + bz) * 2 + bc

    lane = lax.broadcasted_iota(jnp.int32, (key_cap, 2 * HDIM), 1)
    slot_ids = lax.broadcasted_iota(jnp.int32, (key_cap, 1), 0)
    total = 0
    for swap, sources in ((0, near_refs), (1, far_refs)):
        for step_z, source in zip(Z_STEPS, sources):

            def place_piece(by, total, swap=swap, step_z=step_z, source=source):
                block = block_of(by, step_z, swap)
                count = key_starts_ref[block + 1] - key_starts_ref[block]
                start = pl.multiple_of(by * key_cap, 16)
                pair = source[pl.ds(start, key_cap), :].astype(jnp.float32)
                valid = slot_ids < count
                target = pl.ds(pl.multiple_of(total, 16), key_cap)
                keys[target, :] = jnp.where(
                    lane < HDIM,
                    pair,
                    jnp.where(lane == HDIM, jnp.where(valid, 0.0, LOW), 0.0),
                ).astype(jnp.bfloat16)
                values[target, :] = jnp.where(
                    lane >= HDIM,
                    pair,
                    jnp.where(lane == 0, jnp.where(valid, 1.0, 0.0), 0.0),
                ).astype(jnp.bfloat16)
                return total + (count + 15) // 16 * 16

            total = lax.fori_loop(0, y_size, place_piece, total)
    tail_lane = lax.broadcasted_iota(jnp.int32, (KCHUNK, 2 * HDIM), 1)
    tail = pl.ds(pl.multiple_of(total, 16), KCHUNK)
    keys[tail, :] = jnp.where(tail_lane == HDIM, LOW, 0.0).astype(jnp.bfloat16)
    values[tail, :] = jnp.zeros((KCHUNK, 2 * HDIM), jnp.bfloat16)

    queries[...] = jnp.zeros_like(queries)
    results[...] = jnp.zeros_like(results)
    q_lane = lax.broadcasted_iota(jnp.int32, (half, 2 * HDIM), 1)
    offsets = []
    offset = 0
    for by in range(y_size):
        block = block_of(by, 0, 0)
        count = query_starts_ref[block + 1] - query_starts_ref[block]
        offsets.append(offset)
        packed = q_ref[by * half : (by + 1) * half, :].astype(jnp.float32) * (HDIM**-0.5)
        rolled = pltpu.roll(packed, HDIM, 1)
        for number, value in ((0, packed), (1, rolled)):
            filled = jnp.where(q_lane < HDIM, value, jnp.where(q_lane == HDIM, 1.0, 0.0))
            queries[pl.ds(pl.multiple_of(offset + number * half, 16), half), :] = filled.astype(
                jnp.bfloat16
            )
        offset = offset + (count + 15) // 16 * 16
    chunks = (total + KCHUNK - 1) // KCHUNK

    def tile_step(tile, unused):
        rows = pl.ds(pl.multiple_of(tile * QTILE, QTILE), QTILE)
        q = queries[rows, :]

        def chunk_step(chunk, state):
            peak, acc = state
            span = pl.ds(pl.multiple_of(chunk * KCHUNK, KCHUNK), KCHUNK)
            scores = lax.dot_general(
                q, keys[span, :], (((1,), (1,)), ((), ())), preferred_element_type=jnp.float32
            )
            new_peak = jnp.maximum(peak, jnp.max(scores, axis=1, keepdims=True))
            weights = jnp.exp(scores - new_peak).astype(jnp.bfloat16)
            acc = acc * jnp.exp(peak - new_peak) + jnp.dot(
                weights, values[span, :], preferred_element_type=jnp.float32
            )
            return new_peak, acc

        _, acc = lax.fori_loop(
            0,
            chunks,
            chunk_step,
            (
                jnp.full((QTILE, 1), LOW, jnp.float32),
                jnp.zeros((QTILE, 2 * HDIM), jnp.float32),
            ),
        )
        results[rows, :] = (acc / acc[:, 0:1]).astype(jnp.bfloat16)
        return unused

    lax.fori_loop(0, (offset + QTILE - 1) // QTILE, tile_step, 0)

    for by in range(y_size):
        first = results[pl.ds(pl.multiple_of(offsets[by], 16), half), :]
        second = results[pl.ds(pl.multiple_of(offsets[by] + half, 16), half), :]
        out_ref[by * half : (by + 1) * half, :] = jnp.concatenate(
            [first[:, HDIM:], second[:, HDIM:]], axis=1
        )


def final_kernel(
    place_ref,
    slots_ref,
    light_ref,
    light_out_ref,
    m0_ref,
    m1_ref,
    m2_ref,
    m3_ref,
    own_ref,
    near_ref,
    near2_ref,
    far_ref,
    far2_ref,
    out_ref,
    mixed,
):
    pc = place_ref[2]
    rows = light_ref.shape[0]
    heads = 4
    half = m0_ref.shape[0] // heads

    @pl.when(pl.program_id(0) == 0)
    def _():
        slots = slots_ref.shape[1]
        token = lax.broadcasted_iota(jnp.int32, (rows, slots), 0)
        place = jnp.where(token == slots_ref[...], 1.0, 0.0).astype(jnp.bfloat16)
        for number, source in enumerate((m0_ref, m1_ref, m2_ref, m3_ref)):
            parts = []
            for position in range(heads):
                head = (position + 2 * pc) % heads if number == 3 else position
                packed = source[pl.ds(pl.multiple_of(head * half, half), half), :]
                parts.append(jnp.concatenate([packed[:, :HDIM], packed[:, HDIM:]], axis=0))
            wide = jnp.concatenate(parts, axis=1)
            mixed[number] = jnp.dot(place, wide, preferred_element_type=jnp.float32).astype(
                jnp.bfloat16
            )

    acc = jnp.dot(light_ref[...], light_out_ref[...], preferred_element_type=jnp.float32)
    acc += jnp.dot(mixed[0], own_ref[...], preferred_element_type=jnp.float32)
    acc += jnp.dot(mixed[1 + pc], near_ref[...], preferred_element_type=jnp.float32)
    acc += jnp.dot(mixed[2 - pc], near2_ref[...], preferred_element_type=jnp.float32)
    far = jnp.concatenate([far_ref[...], far2_ref[...]], axis=0)
    acc += jnp.dot(mixed[3], far, preferred_element_type=jnp.float32)
    out_ref[...] = acc.astype(out_ref.dtype)


def layer(
    tokens,
    query_index,
    key_index,
    light_query,
    light_key,
    light_value,
    light_out,
    heavy_query,
    heavy_key,
    heavy_value,
    heavy_out,
):
    rows, model = tokens.shape
    y_size, z_size, x_size = lax.axis_size("y"), lax.axis_size("z"), lax.axis_size("x")
    blocks = y_size * z_size * 2
    block_len = rows * x_size
    py, pz, pc, px = (lax.axis_index(a) for a in ALL_AXES)
    block = (py * z_size + pz) * 2 + pc
    first = (block * x_size + px) * rows
    query_cap = block_len // 4
    key_cap = 3 * block_len // 32
    quarter = key_cap // x_size
    width = light_query.shape[1]
    heavy_width = heavy_query.shape[1]
    bf16 = jnp.bfloat16
    place = jnp.stack([py, pz, pc, px, block * block_len, first]).astype(jnp.int32)
    key_lines = key_index.reshape(-1, 128)
    query_lines = query_index.reshape(-1, 128)

    def array(*shape):
        return jax.ShapeDtypeStruct(shape, bf16)

    wq = gather_weights(heavy_query)

    picked = pl.pallas_call(
        pick_kernel,
        out_shape=[array(quarter, model)] * x_size,
        in_specs=[smem()] + [vmem()] * 2,
        out_specs=[vmem()] * x_size,
        scratch_shapes=[pltpu.VMEM((key_cap, model), bf16)],
        cost_estimate=cost(2 * key_cap * rows * model, 2 * rows * model),
        name="pick",
    )(place, key_lines, tokens)
    arrived = [shift(picked[step], "x", step) for step in (1, 3, 2)]
    piece = picked[0] + arrived[0] + arrived[1] + arrived[2]
    row_pieces = [piece] + [shift(piece, "x", step) for step in (1, 2, 3)]

    light_rows, light_pair, head, tail = pl.pallas_call(
        local_kernel,
        out_shape=[array(rows, width), array(rows, 2 * width)] + [array(HALO, 2 * width)] * 2,
        in_specs=[vmem()] * 4,
        out_specs=[vmem()] * 4,
        cost_estimate=cost(6 * rows * width * model, 2 * rows * model + 6 * model * width),
        name="light_project",
    )(tokens, light_query, light_key, light_value)
    devices = blocks * x_size
    up = [(i, i + 1) for i in range(devices - 1)]
    before = lax.ppermute(tail, ALL_AXES, up)
    after = lax.ppermute(head, ALL_AXES, [(b, a) for a, b in up])
    light_mixed = pl.pallas_call(
        functools.partial(light_kernel, total=rows * devices),
        out_shape=array(rows, width),
        in_specs=[smem()] + [vmem()] * 4,
        out_specs=vmem(),
        scratch_shapes=[pltpu.VMEM((rows + 2 * HALO, 2 * width), bf16)],
        cost_estimate=cost(4 * rows * 512 * 256 * 4, 4 * rows * width * 2, 4 * rows * 512),
        name="light",
    )(first.reshape(1), light_rows, before, light_pair, after)

    bounds = jnp.arange(blocks + 1, dtype=jnp.int32) * block_len
    key_starts = jnp.sum((key_index[None, :] < bounds[:, None]).astype(jnp.int32), axis=1)
    query_starts = jnp.sum((query_index[None, :] < bounds[:, None]).astype(jnp.int32), axis=1)

    pairs = pl.pallas_call(
        pair_kernel,
        out_shape=array(y_size * key_cap, 2 * HDIM),
        in_specs=[smem()] + [vmem()] * 6,
        out_specs=vmem(),
        scratch_shapes=[pltpu.VMEM((key_cap, model), bf16)],
        cost_estimate=cost(4 * key_cap * model * heavy_width, 4 * model * heavy_width),
        name="key_value_heads",
    )(place, *row_pieces, heavy_key, heavy_value)
    column = exchange(pairs)

    *projected, query_slots = pl.pallas_call(
        project_kernel,
        out_shape=[array(query_cap, heavy_width)] * x_size
        + [jax.ShapeDtypeStruct((1, query_cap), jnp.int32)],
        in_specs=[smem()] + [vmem()] * 7,
        out_specs=[vmem()] * (x_size + 1),
        scratch_shapes=[
            pltpu.VMEM((model, heavy_width), bf16),
            pltpu.VMEM((x_size, rows, heavy_width), bf16),
        ],
        cost_estimate=cost(8 * query_cap * model * heavy_width, 8 * model * heavy_width),
        name="query_project",
    )(place, query_lines, tokens, heavy_query, *wq)
    q_in = [shift(projected[i + 1], "x", step) for i, step in enumerate((-1, 1, 2))]
    q_heads = pl.pallas_call(
        query_kernel,
        out_shape=array(y_size * query_cap // 2, 2 * HDIM),
        in_specs=[vmem()] * 4,
        out_specs=vmem(),
        cost_estimate=cost(4 * query_cap * heavy_width, 10 * query_cap * heavy_width),
        name="query_heads",
    )(projected[0], *q_in)
    q_column = exchange(q_heads)

    wo = gather_weights(heavy_out)

    ring = {0: column}
    for step in range(1, z_size // 2 + 1):
        ring[-step] = shift(ring[-step + 1], "z", 1)
        if step < z_size // 2:
            ring[step] = shift(ring[step - 1], "z", -1)
    near_pairs = [ring[s] for s in Z_STEPS]
    far_pairs = [shift(ring[s], "c", 1) for s in Z_STEPS]

    key_total = 2 * z_size * column.shape[0]
    slots_total = y_size * query_cap + QTILE
    heads_out = pl.pallas_call(
        functools.partial(attention_kernel, sizes=(y_size, z_size)),
        out_shape=array(y_size * query_cap // 2, 2 * HDIM),
        in_specs=[smem()] * 3 + [vmem()] * (1 + 2 * z_size),
        out_specs=vmem(),
        scratch_shapes=[
            pltpu.VMEM((slots_total, 2 * HDIM), bf16),
            pltpu.VMEM((key_total + KCHUNK, 2 * HDIM), bf16),
            pltpu.VMEM((key_total + KCHUNK, 2 * HDIM), bf16),
            pltpu.VMEM((slots_total, 2 * HDIM), bf16),
        ],
        cost_estimate=cost(4 * 1024 * key_total * 256, 4 * key_total * HDIM, 1024 * key_total),
        name="heavy_attention",
    )(place, query_starts, key_starts, q_column, *near_pairs, *far_pairs)

    back = exchange(heads_out)
    groups = [back] + [shift(back, "x", step) for step in (1, -1, 2)]
    tile = 512

    def whole(*shape):
        return pl.BlockSpec(shape, lambda j: (0,) * len(shape))

    def columns(count):
        return pl.BlockSpec((count, tile), lambda j: (0, j))

    return pl.pallas_call(
        final_kernel,
        grid=(model // tile,),
        out_shape=array(rows, model),
        in_specs=[smem(), whole(1, query_cap), whole(rows, width), columns(width)]
        + [whole(y_size * query_cap // 2, 2 * HDIM)] * 4
        + [columns(heavy_width)]
        + [columns(p.shape[0]) for p in wo],
        out_specs=columns(rows),
        scratch_shapes=[pltpu.VMEM((4, rows, heavy_width), bf16)],
        cost_estimate=cost(2 * rows * 1280 * model, 10 * rows * model),
        name="combine",
    )(
        place,
        query_slots,
        light_mixed,
        light_out,
        *groups,
        heavy_out,
        *wo,
    )


def solution(mesh):
    torus = Mesh(mesh.devices.reshape(4, 8, 2, mesh.shape["head"]), ALL_AXES)
    return jax.shard_map(
        layer,
        mesh=torus,
        in_specs=(P(ALL_AXES, None),)
        + (P(),) * 6
        + (P(None, "x"),) * 3
        + (P("x", None),),
        out_specs=P(ALL_AXES, None),
        check_vma=False,
    )
```

profile of v0, /device:TPU:14, one launch (start us, length us, event | category | flops | bytes accessed | tf_op | source)
XLA Modules:
  0.0 181.9 jit_solution(17602157881040504088)
XLA Ops:
  1.1 3.4 %pick.1 = (bf16[48,2048]{1,0:T(8,128)(2,1)}, bf16[48,2048]{1,0:T(8,128)(2,1)}, bf16[48,2048]{1,0:T(8,128)(2,1)}, bf16[48,2048]{1,0:T(8,128)(2,1)}) custom-call(s32[6]{0:T(128)} %stack.27.place_ref, s32[64,128]{1,0:T(8,128)} %bitcast.26, bf16[512,2048]{1,0:T(8,128)(2,1)} %tokens_ref.5), custom_call_target="tpu_custom_call" | custom-call | flops 402653184 | bytes 2097152 | tf_op jit(solution)/shard_map/pick/pallas_call | solution.py:402
  4.5 2.4 %collective-permute-start.11 = (bf16[48,2048]{1,0:T(8,128)(2,1)}, bf16[48,2048]{1,0:T(8,128)(2,1)S(1)}, u32[]{:S(2)}, u32[]{:S(2)}) collective-permute-start(bf16[48,2048]{1,0:T(8,128)(2,1)} %get-tuple-element.30), channel_id=1, source_target_pairs={{0,2},{1,3},{2,0},{3,1},{4,6},{5,7},{6,4},{7,5},{8,10},{9,11},{10,... | collective-permute-start | bytes 589832 | tf_op jit(solution)/shard_map/ppermute | solution.py:24
  6.9 3.2 %collective-permute-start.9 = (bf16[48,2048]{1,0:T(8,128)(2,1)}, bf16[48,2048]{1,0:T(8,128)(2,1)S(1)}, u32[]{:S(2)}, u32[]{:S(2)}) collective-permute-start(bf16[48,2048]{1,0:T(8,128)(2,1)} %get-tuple-element.28), channel_id=1, source_target_pairs={{0,1},{1,2},{2,3},{3,0},{4,5},{5,6},{6,7},{7,4},{8,9},{9,10},{10,1... | collective-permute-start | bytes 589832 | tf_op jit(solution)/shard_map/ppermute | solution.py:24
  10.2 9.1 %collective-permute-done.near_ref = bf16[2048,256]{1,0:T(8,128)(2,1)S(1)} collective-permute-done((bf16[2048,256]{1,0:T(8,128)(2,1)}, bf16[2048,256]{1,0:T(8,128)(2,1)S(1)}, u32[]{:S(2)}, u32[]{:S(2)}) %collective-permute-start) | collective-permute-done | bytes 1048608 | tf_op jit(solution)/shard_map/ppermute | solution.py:31
  28.6 6.8 %collective-permute-done.12.a_ref = bf16[48,2048]{1,0:T(8,128)(2,1)S(1)} collective-permute-done((bf16[48,2048]{1,0:T(8,128)(2,1)S(1)}, bf16[48,2048]{1,0:T(8,128)(2,1)S(1)}, u32[]{:S(2)}, u32[]{:S(2)}) %collective-permute-start.12) | collective-permute-done | bytes 196640 | tf_op jit(solution)/shard_map/ppermute | solution.py:24
  36.2 8.4 %collective-permute-done.14.c_ref = bf16[48,2048]{1,0:T(8,128)(2,1)S(1)} collective-permute-done((bf16[48,2048]{1,0:T(8,128)(2,1)S(1)}, bf16[48,2048]{1,0:T(8,128)(2,1)S(1)}, u32[]{:S(2)}, u32[]{:S(2)}) %collective-permute-start.14) | collective-permute-done | bytes 196640 | tf_op jit(solution)/shard_map/ppermute | solution.py:24
  45.3 3.3 %key_value_heads.1 = bf16[768,128]{1,0:T(8,128)(2,1)} custom-call(s32[6]{0:T(128)} %stack.27.place_ref, bf16[48,2048]{1,0:T(8,128)(2,1)} %copy-done, bf16[48,2048]{1,0:T(8,128)(2,1)} %copy-done.8, bf16[48,2048]{1,0:T(8,128)(2,1)} %copy-done.9, bf16[48,2048]{1,0:T(8,128)(2,1)} %copy-done.10, bf16[2048,256]{1,0:T(8,128)(2,1)} %key_ref.3, ...), custom_call_target="tpu_custom_call" | custom-call | flops 402653184 | bytes 2097152 | tf_op jit(solution)/shard_map/key_value_heads/pallas_call | solution.py:441
  48.5 7.9 %all-to-all-start.1 = ((bf16[4,192,128]{2,1,0:T(8,128)(2,1)}), bf16[4,192,128]{2,1,0:T(8,128)(2,1)S(1)}, u32[]{:S(2)}, u32[]{:S(2)}) async-start(bf16[4,192,128]{2,1,0:T(8,128)(2,1)} %bitcast.15), calls=%async_computation.1 | async-start | bytes 393216 | tf_op jit(solution)/shard_map/all_to_all | solution.py:213
  56.4 2.1 %collective-permute-start.3 = (bf16[1024,256]{1,0:T(8,128)(2,1)}, bf16[1024,256]{1,0:T(8,128)(2,1)S(1)}, u32[]{:S(2)}, u32[]{:S(2)}) collective-permute-start(bf16[1024,256]{1,0:T(8,128)(2,1)} %collective-permute-done.2.far_ref), channel_id=1, source_target_pairs={{0,4},{4,0},{1,5},{5,1},{2,6},{6,2},{3,7},{7,3},{8,12},{12,8},{9,1... | collective-permute-start | bytes 1572872 | tf_op jit(solution)/shard_map/ppermute | solution.py:24
  58.6 2.8 %all-to-all-done.1 = bf16[4,192,128]{2,1,0:T(8,128)(2,1)S(1)} async-done(((bf16[4,192,128]{2,1,0:T(8,128)(2,1)}), bf16[4,192,128]{2,1,0:T(8,128)(2,1)S(1)}, u32[]{:S(2)}, u32[]{:S(2)}) %all-to-all-start.1) | async-done | bytes 196640 | tf_op jit(solution)/shard_map/all_to_all | solution.py:213
  61.3 3.2 %collective-permute-start.16 = (bf16[768,128]{1,0:T(8,128)(2,1)S(1)}, bf16[768,128]{1,0:T(8,128)(2,1)S(1)}, u32[]{:S(2)}, u32[]{:S(2)}) collective-permute-start(bf16[768,128]{1,0:T(8,128)(2,1)S(1)} %bitcast.23), channel_id=1, source_target_pairs={{0,56},{8,0},{16,8},{24,16},{32,24},{40,32},{48,40},{56,48},{1,57}... | collective-permute-start | bytes 589832 | tf_op jit(solution)/shard_map/ppermute | solution.py:24
  64.6 3.6 %collective-permute-done.15.refs_2_ = bf16[768,128]{1,0:T(8,128)(2,1)S(1)} collective-permute-done((bf16[768,128]{1,0:T(8,128)(2,1)S(1)}, bf16[768,128]{1,0:T(8,128)(2,1)S(1)}, u32[]{:S(2)}, u32[]{:S(2)}) %collective-permute-start.15) | collective-permute-done | bytes 196640 | tf_op jit(solution)/shard_map/ppermute | solution.py:24
  68.2 3.1 %collective-permute-start.22 = (bf16[768,128]{1,0:T(8,128)(2,1)S(1)}, bf16[768,128]{1,0:T(8,128)(2,1)S(1)}, u32[]{:S(2)}, u32[]{:S(2)}) collective-permute-start(bf16[768,128]{1,0:T(8,128)(2,1)S(1)} %bitcast.24), channel_id=1, source_target_pairs={{0,4},{4,0},{1,5},{5,1},{2,6},{6,2},{3,7},{7,3},{8,12},{12,8},{9,1... | collective-permute-start | bytes 589832 | tf_op jit(solution)/shard_map/ppermute | solution.py:24
  71.3 4.0 %collective-permute-done.17.refs_4_ = bf16[768,128]{1,0:T(8,128)(2,1)} collective-permute-done((bf16[768,128]{1,0:T(8,128)(2,1)S(1)}, bf16[768,128]{1,0:T(8,128)(2,1)}, u32[]{:S(2)}, u32[]{:S(2)}) %collective-permute-start.17) | collective-permute-done | bytes 196640 | tf_op jit(solution)/shard_map/ppermute | solution.py:24
  79.2 7.2 %query_project.1 = (bf16[512,256]{1,0:T(8,128)(2,1)}, bf16[512,256]{1,0:T(8,128)(2,1)}, bf16[512,256]{1,0:T(8,128)(2,1)}, bf16[512,256]{1,0:T(8,128)(2,1)}, s32[1,512]{1,0:T(1,128)}) custom-call(s32[6]{0:T(128)} %stack.27.place_ref, s32[64,128]{1,0:T(8,128)} %bitcast.27, bf16[512,2048]{1,0:T(8,128)(2,1)} %tokens_ref.5, bf16[2048,256]{1,0:T(8,128)(2,1)} %own_ref.2, ...), custom_call_target="tpu_custom_call" | custom-call | flops 2147483648 | bytes 4194304 | tf_op jit(solution)/shard_map/query_project/pallas_call | solution.py:452
  86.4 3.6 %collective-permute-start.6 = (bf16[512,256]{1,0:T(8,128)(2,1)}, bf16[512,256]{1,0:T(8,128)(2,1)S(1)}, u32[]{:S(2)}, u32[]{:S(2)}) collective-permute-start(bf16[512,256]{1,0:T(8,128)(2,1)} %get-tuple-element.24), channel_id=1, source_target_pairs={{0,3},{1,0},{2,1},{3,2},{4,7},{5,4},{6,5},{7,6},{8,11},{9,8},{10,9... | collective-permute-start | bytes 786440 | tf_op jit(solution)/shard_map/ppermute | solution.py:24
  90.6 3.3 %collective-permute-start.7 = (bf16[512,256]{1,0:T(8,128)(2,1)}, bf16[512,256]{1,0:T(8,128)(2,1)S(1)}, u32[]{:S(2)}, u32[]{:S(2)}) collective-permute-start(bf16[512,256]{1,0:T(8,128)(2,1)} %get-tuple-element.25), channel_id=1, source_target_pairs={{0,1},{1,2},{2,3},{3,0},{4,5},{5,6},{6,7},{7,4},{8,9},{9,10},{10,1... | collective-permute-start | bytes 786440 | tf_op jit(solution)/shard_map/ppermute | solution.py:24
  96.1 4.5 %collective-permute-done.6.a_ref = bf16[512,256]{1,0:T(8,128)(2,1)S(1)} collective-permute-done((bf16[512,256]{1,0:T(8,128)(2,1)}, bf16[512,256]{1,0:T(8,128)(2,1)S(1)}, u32[]{:S(2)}, u32[]{:S(2)}) %collective-permute-start.6) | collective-permute-done | bytes 262176 | tf_op jit(solution)/shard_map/ppermute | solution.py:24
  100.6 3.0 %collective-permute-start.20 = (bf16[768,128]{1,0:T(8,128)(2,1)}, bf16[768,128]{1,0:T(8,128)(2,1)}, u32[]{:S(2)}, u32[]{:S(2)}) collective-permute-start(bf16[768,128]{1,0:T(8,128)(2,1)} %copy-done.22), channel_id=1, source_target_pairs={{0,56},{8,0},{16,8},{24,16},{32,24},{40,32},{48,40},{56,48},{1,57}... | collective-permute-start | bytes 589832 | tf_op jit(solution)/shard_map/ppermute | solution.py:24
  103.6 2.2 %collective-permute-done.7.b_ref = bf16[512,256]{1,0:T(8,128)(2,1)S(1)} collective-permute-done((bf16[512,256]{1,0:T(8,128)(2,1)}, bf16[512,256]{1,0:T(8,128)(2,1)S(1)}, u32[]{:S(2)}, u32[]{:S(2)}) %collective-permute-start.7) | collective-permute-done | bytes 262176 | tf_op jit(solution)/shard_map/ppermute | solution.py:24
  110.5 4.8 %all-to-all-start = ((bf16[4,256,128]{2,1,0:T(8,128)(2,1)}), bf16[4,256,128]{2,1,0:T(8,128)(2,1)S(1)}, u32[]{:S(2)}, u32[]{:S(2)}) async-start(bf16[4,256,128]{2,1,0:T(8,128)(2,1)} %bitcast.14), calls=%async_computation | async-start | bytes 524288 | tf_op jit(solution)/shard_map/all_to_all | solution.py:213
  121.2 13.1 %heavy_attention.1 = bf16[1024,128]{1,0:T(8,128)(2,1)} custom-call(s32[6]{0:T(128)} %stack.27.place_ref, s32[65]{0:T(128)} %get-tuple-element.32.query_starts_ref, s32[65]{0:T(128)} %get-tuple-element.31.key_starts_ref, bf16[1024,128]{1,0:T(8,128)(2,1)} %bitcast.16, bf16[768,128]{1,0:T(8,128)(2,1)} %bitcast.25, bf16[768,128]{1,0:T(8,128)(2,1)} %copy-done.19, ...), custom_call_target="tpu_custom_call" | custom-call | flops 12884901888 | bytes 3145728 | tf_op jit(solution)/shard_map/heavy_attention/pallas_call | solution.py:488
  134.3 4.8 %all-to-all-start.2 = ((bf16[4,256,128]{2,1,0:T(8,128)(2,1)}), bf16[4,256,128]{2,1,0:T(8,128)(2,1)S(1)}, u32[]{:S(2)}, u32[]{:S(2)}) async-start(bf16[4,256,128]{2,1,0:T(8,128)(2,1)} %bitcast.21), calls=%async_computation.2 | async-start | bytes 524288 | tf_op jit(solution)/shard_map/all_to_all | solution.py:213
  139.2 5.3 %light_project.1 = (bf16[512,256]{1,0:T(8,128)(2,1)}, bf16[512,512]{1,0:T(8,128)(2,1)}, bf16[128,512]{1,0:T(8,128)(2,1)}, bf16[128,512]{1,0:T(8,128)(2,1)}) custom-call(bf16[512,2048]{1,0:T(8,128)(2,1)} %tokens_ref.5, bf16[2048,256]{1,0:T(8,128)(2,1)} %query_ref.1, bf16[2048,256]{1,0:T(8,128)(2,1)} %key_ref.2, bf16[2048,256]{1,0:T(8,128)(2,1)} %value_ref.2), custom_call_target="tpu_custom_call" | custom-call | flops 1610612736 | bytes 5242880 | tf_op jit(solution)/shard_map/light_project/pallas_call | solution.py:415
  144.5 3.5 %collective-permute-start.4 = (bf16[128,512]{1,0:T(8,128)(2,1)}, bf16[128,512]{1,0:T(8,128)(2,1)}, u32[]{:S(2)}, u32[]{:S(2)}) collective-permute-start(bf16[128,512]{1,0:T(8,128)(2,1)} %get-tuple-element.20), channel_id=1, source_target_pairs={{0,1},{1,2},{2,3},{3,4},{4,5},{5,6},{6,7},{7,8},{8,9},{9,10},{10,1... | collective-permute-start | bytes 393224 | tf_op jit(solution)/shard_map/ppermute | solution.py:425
  148.0 2.4 %collective-permute-start.5 = (bf16[128,512]{1,0:T(8,128)(2,1)}, bf16[128,512]{1,0:T(8,128)(2,1)}, u32[]{:S(2)}, u32[]{:S(2)}) collective-permute-start(bf16[128,512]{1,0:T(8,128)(2,1)} %get-tuple-element.22), channel_id=1, source_target_pairs={{1,0},{2,1},{3,2},{4,3},{5,4},{6,5},{7,6},{8,7},{9,8},{10,9},{11,1... | collective-permute-start | bytes 393224 | tf_op jit(solution)/shard_map/ppermute | solution.py:426
  150.4 6.7 %collective-permute-start.30 = (bf16[1024,128]{1,0:T(8,128)(2,1)S(1)}, bf16[1024,128]{1,0:T(8,128)(2,1)S(1)}, u32[]{:S(2)}, u32[]{:S(2)}) collective-permute-start(bf16[1024,128]{1,0:T(8,128)(2,1)S(1)} %bitcast.17), channel_id=1, source_target_pairs={{0,1},{1,2},{2,3},{3,0},{4,5},{5,6},{6,7},{7,4},{8,9},{9,10},{10,1... | collective-permute-start | bytes 786440 | tf_op jit(solution)/shard_map/ppermute | solution.py:24
  157.1 2.5 %collective-permute-start.32 = (bf16[1024,128]{1,0:T(8,128)(2,1)S(1)}, bf16[1024,128]{1,0:T(8,128)(2,1)}, u32[]{:S(2)}, u32[]{:S(2)}) collective-permute-start(bf16[1024,128]{1,0:T(8,128)(2,1)S(1)} %bitcast.19), channel_id=1, source_target_pairs={{0,2},{1,3},{2,0},{3,1},{4,6},{5,7},{6,4},{7,5},{8,10},{9,11},{10,... | collective-permute-start | bytes 786440 | tf_op jit(solution)/shard_map/ppermute | solution.py:24
  159.5 4.2 %light.1.light_ref = bf16[512,256]{1,0:T(8,128)(2,1)} custom-call(s32[1]{0:T(128)} %bitcast.5.first_ref, bf16[512,256]{1,0:T(8,128)(2,1)} %get-tuple-element.19.q_ref, bf16[128,512]{1,0:T(8,128)(2,1)} %collective-permute-done.4.prev_ref, bf16[512,512]{1,0:T(8,128)(2,1)} %get-tuple-element.21.own_ref, bf16[128,512]{1,0:T(8,128)(2,1)} %collective-permute-done.5.next_ref), custom_call_target="tpu_custom_call" | custom-call | flops 1073741824 | bytes 1048576 | tf_op jit(solution)/shard_map/light/pallas_call | solution.py:427
  163.8 4.7 %collective-permute-done.30.m1_ref = bf16[1024,128]{1,0:T(8,128)(2,1)S(1)} collective-permute-done((bf16[1024,128]{1,0:T(8,128)(2,1)S(1)}, bf16[1024,128]{1,0:T(8,128)(2,1)S(1)}, u32[]{:S(2)}, u32[]{:S(2)}) %collective-permute-start.30) | collective-permute-done | bytes 262176 | tf_op jit(solution)/shard_map/ppermute | solution.py:24
  168.5 5.0 %collective-permute-done.31.m2_ref = bf16[1024,128]{1,0:T(8,128)(2,1)S(1)} collective-permute-done((bf16[1024,128]{1,0:T(8,128)(2,1)S(1)}, bf16[1024,128]{1,0:T(8,128)(2,1)S(1)}, u32[]{:S(2)}, u32[]{:S(2)}) %collective-permute-start.31) | collective-permute-done | bytes 262176 | tf_op jit(solution)/shard_map/ppermute | solution.py:24
  174.2 7.7 %combine.1 = bf16[512,2048]{1,0:T(8,128)(2,1)} custom-call(s32[6]{0:T(128)} %stack.27.place_ref, s32[1,512]{1,0:T(1,128)} %get-tuple-element.18.slots_ref, bf16[512,256]{1,0:T(8,128)(2,1)} %light.1.light_ref, bf16[256,2048]{1,0:T(8,128)(2,1)} %light_out_ref.1, bf16[1024,128]{1,0:T(8,128)(2,1)} %bitcast.20, bf16[1024,128]{1,0:T(8,128)(2,1)} %copy-done.17, ...), custom_call_target="tpu_custom_call" | custom-call | flops 2684354560 | bytes 10485760 | tf_op jit(solution)/shard_map/combine/pallas_call | solution.py:513
  (116 shorter events, 30.0 us)
Async XLA Ops:
  0.0 19.2 %collective-permute-start = (bf16[2048,256]{1,0:T(8,128)(2,1)}, bf16[2048,256]{1,0:T(8,128)(2,1)S(1)}, u32[]{:S(2)}, u32[]{:S(2)}) collective-permute-start(bf16[2048,256]{1,0:T(8,128)(2,1)} %own_ref.2), channel_id=1, source_target_pairs={{0,1},{1,2},{2,3},{3,0},{4,7},{5,4},{6,5},{7,6},{8,9},{9,10},{10,1... | collective-permute-start | bytes 3145736 | tf_op jit(solution)/shard_map/ppermute | solution.py:31
  4.5 16.9 %collective-permute-start.11 = (bf16[48,2048]{1,0:T(8,128)(2,1)}, bf16[48,2048]{1,0:T(8,128)(2,1)S(1)}, u32[]{:S(2)}, u32[]{:S(2)}) collective-permute-start(bf16[48,2048]{1,0:T(8,128)(2,1)} %get-tuple-element.30), channel_id=1, source_target_pairs={{0,2},{1,3},{2,0},{3,1},{4,6},{5,7},{6,4},{7,5},{8,10},{9,11},{10,... | collective-permute-start | bytes 589832 | tf_op jit(solution)/shard_map/ppermute | solution.py:24
  6.9 14.5 %collective-permute-start.10 = (bf16[48,2048]{1,0:T(8,128)(2,1)}, bf16[48,2048]{1,0:T(8,128)(2,1)S(1)}, u32[]{:S(2)}, u32[]{:S(2)}) collective-permute-start(bf16[48,2048]{1,0:T(8,128)(2,1)} %get-tuple-element.29), channel_id=1, source_target_pairs={{0,3},{1,0},{2,1},{3,2},{4,7},{5,4},{6,5},{7,6},{8,11},{9,8},{10,9... | collective-permute-start | bytes 589832 | tf_op jit(solution)/shard_map/ppermute | solution.py:24
  6.9 16.6 %collective-permute-start.9 = (bf16[48,2048]{1,0:T(8,128)(2,1)}, bf16[48,2048]{1,0:T(8,128)(2,1)S(1)}, u32[]{:S(2)}, u32[]{:S(2)}) collective-permute-start(bf16[48,2048]{1,0:T(8,128)(2,1)} %get-tuple-element.28), channel_id=1, source_target_pairs={{0,1},{1,2},{2,3},{3,0},{4,5},{5,6},{6,7},{7,4},{8,9},{9,10},{10,1... | collective-permute-start | bytes 589832 | tf_op jit(solution)/shard_map/ppermute | solution.py:24
  19.3 37.2 %collective-permute-start.2 = (bf16[1024,256]{1,0:T(8,128)(2,1)S(1)}, bf16[1024,256]{1,0:T(8,128)(2,1)}, u32[]{:S(2)}, u32[]{:S(2)}) collective-permute-start(bf16[1024,256]{1,0:T(8,128)(2,1)S(1)} %constant_dynamic-slice_fusion.1), channel_id=1, source_target_pairs={{0,1},{1,2},{2,3},{3,0},{4,7},{5,4},{6,5},{7,6},{8,9},{9,10},{10,1... | collective-permute-start | bytes 1572872 | tf_op jit(solution)/shard_map/ppermute | solution.py:31
  21.0 56.1 %collective-permute-start.1 = (bf16[2048,256]{1,0:T(8,128)(2,1)S(1)}, bf16[2048,256]{1,0:T(8,128)(2,1)}, u32[]{:S(2)}, u32[]{:S(2)}) collective-permute-start(bf16[2048,256]{1,0:T(8,128)(2,1)S(1)} %collective-permute-done.near_ref), channel_id=1, source_target_pairs={{0,4},{4,0},{1,5},{5,1},{2,6},{6,2},{3,7},{7,3},{8,12},{12,8},{9,1... | collective-permute-start | bytes 3145736 | tf_op jit(solution)/shard_map/ppermute | solution.py:24
  24.5 11.0 %collective-permute-start.12 = (bf16[48,2048]{1,0:T(8,128)(2,1)S(1)}, bf16[48,2048]{1,0:T(8,128)(2,1)S(1)}, u32[]{:S(2)}, u32[]{:S(2)}) collective-permute-start(bf16[48,2048]{1,0:T(8,128)(2,1)S(1)} %add_add_fusion.own_ref), channel_id=1, source_target_pairs={{0,1},{1,2},{2,3},{3,0},{4,5},{5,6},{6,7},{7,4},{8,9},{9,10},{10,1... | collective-permute-start | bytes 589832 | tf_op jit(solution)/shard_map/ppermute | solution.py:24
  26.2 67.8 %collective-permute-start.33 = (bf16[256,2048]{1,0:T(8,128)(2,1)}, bf16[256,2048]{1,0:T(8,128)(2,1)S(1)}, u32[]{:S(2)}, u32[]{:S(2)}) collective-permute-start(bf16[256,2048]{1,0:T(8,128)(2,1)} %own_ref.3), channel_id=1, source_target_pairs={{0,1},{1,2},{2,3},{3,0},{4,7},{5,4},{6,5},{7,6},{8,9},{9,10},{10,1... | collective-permute-start | bytes 3145736 | tf_op jit(solution)/shard_map/ppermute | solution.py:31
  26.5 9.7 %collective-permute-start.13 = (bf16[48,2048]{1,0:T(8,128)(2,1)S(1)}, bf16[48,2048]{1,0:T(8,128)(2,1)S(1)}, u32[]{:S(2)}, u32[]{:S(2)}) collective-permute-start(bf16[48,2048]{1,0:T(8,128)(2,1)S(1)} %add_add_fusion.own_ref), channel_id=1, source_target_pairs={{0,2},{1,3},{2,0},{3,1},{4,6},{5,7},{6,4},{7,5},{8,10},{9,11},{10,... | collective-permute-start | bytes 589832 | tf_op jit(solution)/shard_map/ppermute | solution.py:24
  35.4 9.2 %collective-permute-start.14 = (bf16[48,2048]{1,0:T(8,128)(2,1)S(1)}, bf16[48,2048]{1,0:T(8,128)(2,1)S(1)}, u32[]{:S(2)}, u32[]{:S(2)}) collective-permute-start(bf16[48,2048]{1,0:T(8,128)(2,1)S(1)} %add_add_fusion.own_ref), channel_id=1, source_target_pairs={{0,3},{1,0},{2,1},{3,2},{4,7},{5,4},{6,5},{7,6},{8,11},{9,8},{10,9... | collective-permute-start | bytes 589832 | tf_op jit(solution)/shard_map/ppermute | solution.py:24
  48.5 12.8 %all-to-all-start.1 = ((bf16[4,192,128]{2,1,0:T(8,128)(2,1)}), bf16[4,192,128]{2,1,0:T(8,128)(2,1)S(1)}, u32[]{:S(2)}, u32[]{:S(2)}) async-start(bf16[4,192,128]{2,1,0:T(8,128)(2,1)} %bitcast.15), calls=%async_computation.1 | async-start | bytes 393216 | tf_op jit(solution)/shard_map/all_to_all | solution.py:213
  56.4 21.4 %collective-permute-start.3 = (bf16[1024,256]{1,0:T(8,128)(2,1)}, bf16[1024,256]{1,0:T(8,128)(2,1)S(1)}, u32[]{:S(2)}, u32[]{:S(2)}) collective-permute-start(bf16[1024,256]{1,0:T(8,128)(2,1)} %collective-permute-done.2.far_ref), channel_id=1, source_target_pairs={{0,4},{4,0},{1,5},{5,1},{2,6},{6,2},{3,7},{7,3},{8,12},{12,8},{9,1... | collective-permute-start | bytes 1572872 | tf_op jit(solution)/shard_map/ppermute | solution.py:24
  68.2 18.1 %collective-permute-start.22 = (bf16[768,128]{1,0:T(8,128)(2,1)S(1)}, bf16[768,128]{1,0:T(8,128)(2,1)S(1)}, u32[]{:S(2)}, u32[]{:S(2)}) collective-permute-start(bf16[768,128]{1,0:T(8,128)(2,1)S(1)} %bitcast.24), channel_id=1, source_target_pairs={{0,4},{4,0},{1,5},{5,1},{2,6},{6,2},{3,7},{7,3},{8,12},{12,8},{9,1... | collective-permute-start | bytes 589832 | tf_op jit(solution)/shard_map/ppermute | solution.py:24
  75.3 20.3 %collective-permute-start.23 = (bf16[768,128]{1,0:T(8,128)(2,1)S(1)}, bf16[768,128]{1,0:T(8,128)(2,1)}, u32[]{:S(2)}, u32[]{:S(2)}) collective-permute-start(bf16[768,128]{1,0:T(8,128)(2,1)S(1)} %collective-permute-done.15.refs_2_), channel_id=1, source_target_pairs={{0,4},{4,0},{1,5},{5,1},{2,6},{6,2},{3,7},{7,3},{8,12},{12,8},{9,1... | collective-permute-start | bytes 589832 | tf_op jit(solution)/shard_map/ppermute | solution.py:24
  77.1 12.8 %collective-permute-start.18 = (bf16[768,128]{1,0:T(8,128)(2,1)S(1)}, bf16[768,128]{1,0:T(8,128)(2,1)S(1)}, u32[]{:S(2)}, u32[]{:S(2)}) collective-permute-start(bf16[768,128]{1,0:T(8,128)(2,1)S(1)} %collective-permute-done.16.refs_3_), channel_id=1, source_target_pairs={{0,56},{8,0},{16,8},{24,16},{32,24},{40,32},{48,40},{56,48},{1,57}... | collective-permute-start | bytes 589832 | tf_op jit(solution)/shard_map/ppermute | solution.py:24
  77.8 18.3 %collective-permute-start.19 = (bf16[768,128]{1,0:T(8,128)(2,1)}, bf16[768,128]{1,0:T(8,128)(2,1)}, u32[]{:S(2)}, u32[]{:S(2)}) collective-permute-start(bf16[768,128]{1,0:T(8,128)(2,1)} %collective-permute-done.17.refs_4_), channel_id=1, source_target_pairs={{0,8},{8,16},{16,24},{24,32},{32,40},{40,48},{48,56},{56,0},{1,9},... | collective-permute-start | bytes 589832 | tf_op jit(solution)/shard_map/ppermute | solution.py:24
  86.4 14.3 %collective-permute-start.6 = (bf16[512,256]{1,0:T(8,128)(2,1)}, bf16[512,256]{1,0:T(8,128)(2,1)S(1)}, u32[]{:S(2)}, u32[]{:S(2)}) collective-permute-start(bf16[512,256]{1,0:T(8,128)(2,1)} %get-tuple-element.24), channel_id=1, source_target_pairs={{0,3},{1,0},{2,1},{3,2},{4,7},{5,4},{6,5},{7,6},{8,11},{9,8},{10,9... | collective-permute-start | bytes 786440 | tf_op jit(solution)/shard_map/ppermute | solution.py:24
  90.6 15.2 %collective-permute-start.7 = (bf16[512,256]{1,0:T(8,128)(2,1)}, bf16[512,256]{1,0:T(8,128)(2,1)S(1)}, u32[]{:S(2)}, u32[]{:S(2)}) collective-permute-start(bf16[512,256]{1,0:T(8,128)(2,1)} %get-tuple-element.25), channel_id=1, source_target_pairs={{0,1},{1,2},{2,3},{3,0},{4,5},{5,6},{6,7},{7,4},{8,9},{9,10},{10,1... | collective-permute-start | bytes 786440 | tf_op jit(solution)/shard_map/ppermute | solution.py:24
  93.9 13.8 %collective-permute-start.8 = (bf16[512,256]{1,0:T(8,128)(2,1)}, bf16[512,256]{1,0:T(8,128)(2,1)S(1)}, u32[]{:S(2)}, u32[]{:S(2)}) collective-permute-start(bf16[512,256]{1,0:T(8,128)(2,1)} %get-tuple-element.26), channel_id=1, source_target_pairs={{0,2},{1,3},{2,0},{3,1},{4,6},{5,7},{6,4},{7,5},{8,10},{9,11},{10,... | collective-permute-start | bytes 786440 | tf_op jit(solution)/shard_map/ppermute | solution.py:24
  95.6 22.3 %collective-permute-start.35 = (bf16[128,2048]{1,0:T(8,128)(2,1)S(1)}, bf16[128,2048]{1,0:T(8,128)(2,1)S(1)}, u32[]{:S(2)}, u32[]{:S(2)}) collective-permute-start(bf16[128,2048]{1,0:T(8,128)(2,1)S(1)} %constant_dynamic-slice_fusion), channel_id=1, source_target_pairs={{0,1},{1,2},{2,3},{3,0},{4,7},{5,4},{6,5},{7,6},{8,9},{9,10},{10,1... | collective-permute-start | bytes 1572872 | tf_op jit(solution)/shard_map/ppermute | solution.py:31
  96.1 19.2 %collective-permute-start.24 = (bf16[768,128]{1,0:T(8,128)(2,1)}, bf16[768,128]{1,0:T(8,128)(2,1)S(1)}, u32[]{:S(2)}, u32[]{:S(2)}) collective-permute-start(bf16[768,128]{1,0:T(8,128)(2,1)} %copy-done.20), channel_id=1, source_target_pairs={{0,4},{4,0},{1,5},{5,1},{2,6},{6,2},{3,7},{7,3},{8,12},{12,8},{9,1... | collective-permute-start | bytes 589832 | tf_op jit(solution)/shard_map/ppermute | solution.py:24
  100.6 14.8 %collective-permute-start.20 = (bf16[768,128]{1,0:T(8,128)(2,1)}, bf16[768,128]{1,0:T(8,128)(2,1)}, u32[]{:S(2)}, u32[]{:S(2)}) collective-permute-start(bf16[768,128]{1,0:T(8,128)(2,1)} %copy-done.22), channel_id=1, source_target_pairs={{0,56},{8,0},{16,8},{24,16},{32,24},{40,32},{48,40},{56,48},{1,57}... | collective-permute-start | bytes 589832 | tf_op jit(solution)/shard_map/ppermute | solution.py:24
  105.8 10.1 %collective-permute-start.25 = (bf16[768,128]{1,0:T(8,128)(2,1)}, bf16[768,128]{1,0:T(8,128)(2,1)}, u32[]{:S(2)}, u32[]{:S(2)}) collective-permute-start(bf16[768,128]{1,0:T(8,128)(2,1)} %collective-permute-done.17.refs_4_), channel_id=1, source_target_pairs={{0,4},{4,0},{1,5},{5,1},{2,6},{6,2},{3,7},{7,3},{8,12},{12,8},{9,1... | collective-permute-start | bytes 589832 | tf_op jit(solution)/shard_map/ppermute | solution.py:24
  110.5 10.1 %all-to-all-start = ((bf16[4,256,128]{2,1,0:T(8,128)(2,1)}), bf16[4,256,128]{2,1,0:T(8,128)(2,1)S(1)}, u32[]{:S(2)}, u32[]{:S(2)}) async-start(bf16[4,256,128]{2,1,0:T(8,128)(2,1)} %bitcast.14), calls=%async_computation | async-start | bytes 524288 | tf_op jit(solution)/shard_map/all_to_all | solution.py:213
  117.7 46.0 %collective-permute-start.34 = (bf16[256,2048]{1,0:T(8,128)(2,1)S(1)}, bf16[256,2048]{1,0:T(8,128)(2,1)S(1)}, u32[]{:S(2)}, u32[]{:S(2)}) collective-permute-start(bf16[256,2048]{1,0:T(8,128)(2,1)S(1)} %collective-permute-done.33.near_ref), channel_id=1, source_target_pairs={{0,4},{4,0},{1,5},{5,1},{2,6},{6,2},{3,7},{7,3},{8,12},{12,8},{9,1... | collective-permute-start | bytes 3145736 | tf_op jit(solution)/shard_map/ppermute | solution.py:24
  117.9 45.9 %collective-permute-start.36 = (bf16[128,2048]{1,0:T(8,128)(2,1)S(1)}, bf16[128,2048]{1,0:T(8,128)(2,1)}, u32[]{:S(2)}, u32[]{:S(2)}) collective-permute-start(bf16[128,2048]{1,0:T(8,128)(2,1)S(1)} %collective-permute-done.35.far_ref), channel_id=1, source_target_pairs={{0,4},{4,0},{1,5},{5,1},{2,6},{6,2},{3,7},{7,3},{8,12},{12,8},{9,1... | collective-permute-start | bytes 1572872 | tf_op jit(solution)/shard_map/ppermute | solution.py:24
  134.3 16.0 %all-to-all-start.2 = ((bf16[4,256,128]{2,1,0:T(8,128)(2,1)}), bf16[4,256,128]{2,1,0:T(8,128)(2,1)S(1)}, u32[]{:S(2)}, u32[]{:S(2)}) async-start(bf16[4,256,128]{2,1,0:T(8,128)(2,1)} %bitcast.21), calls=%async_computation.2 | async-start | bytes 524288 | tf_op jit(solution)/shard_map/all_to_all | solution.py:213
  144.5 12.6 %collective-permute-start.4 = (bf16[128,512]{1,0:T(8,128)(2,1)}, bf16[128,512]{1,0:T(8,128)(2,1)}, u32[]{:S(2)}, u32[]{:S(2)}) collective-permute-start(bf16[128,512]{1,0:T(8,128)(2,1)} %get-tuple-element.20), channel_id=1, source_target_pairs={{0,1},{1,2},{2,3},{3,4},{4,5},{5,6},{6,7},{7,8},{8,9},{9,10},{10,1... | collective-permute-start | bytes 393224 | tf_op jit(solution)/shard_map/ppermute | solution.py:425
  148.0 9.1 %collective-permute-start.5 = (bf16[128,512]{1,0:T(8,128)(2,1)}, bf16[128,512]{1,0:T(8,128)(2,1)}, u32[]{:S(2)}, u32[]{:S(2)}) collective-permute-start(bf16[128,512]{1,0:T(8,128)(2,1)} %get-tuple-element.22), channel_id=1, source_target_pairs={{1,0},{2,1},{3,2},{4,3},{5,4},{6,5},{7,6},{8,7},{9,8},{10,9},{11,1... | collective-permute-start | bytes 393224 | tf_op jit(solution)/shard_map/ppermute | solution.py:426
  150.4 18.1 %collective-permute-start.30 = (bf16[1024,128]{1,0:T(8,128)(2,1)S(1)}, bf16[1024,128]{1,0:T(8,128)(2,1)S(1)}, u32[]{:S(2)}, u32[]{:S(2)}) collective-permute-start(bf16[1024,128]{1,0:T(8,128)(2,1)S(1)} %bitcast.17), channel_id=1, source_target_pairs={{0,1},{1,2},{2,3},{3,0},{4,5},{5,6},{6,7},{7,4},{8,9},{9,10},{10,1... | collective-permute-start | bytes 786440 | tf_op jit(solution)/shard_map/ppermute | solution.py:24
  157.1 16.4 %collective-permute-start.31 = (bf16[1024,128]{1,0:T(8,128)(2,1)S(1)}, bf16[1024,128]{1,0:T(8,128)(2,1)S(1)}, u32[]{:S(2)}, u32[]{:S(2)}) collective-permute-start(bf16[1024,128]{1,0:T(8,128)(2,1)S(1)} %bitcast.18), channel_id=1, source_target_pairs={{0,3},{1,0},{2,1},{3,2},{4,7},{5,4},{6,5},{7,6},{8,11},{9,8},{10,9... | collective-permute-start | bytes 786440 | tf_op jit(solution)/shard_map/ppermute | solution.py:24
  157.1 16.4 %collective-permute-start.32 = (bf16[1024,128]{1,0:T(8,128)(2,1)S(1)}, bf16[1024,128]{1,0:T(8,128)(2,1)}, u32[]{:S(2)}, u32[]{:S(2)}) collective-permute-start(bf16[1024,128]{1,0:T(8,128)(2,1)S(1)} %bitcast.19), channel_id=1, source_target_pairs={{0,2},{1,3},{2,0},{3,1},{4,6},{5,7},{6,4},{7,5},{8,10},{9,11},{10,... | collective-permute-start | bytes 786440 | tf_op jit(solution)/shard_map/ppermute | solution.py:24
  (35 other events, 393.4 us)
where the time goes:
time: 182 us
  starting transfers between devices  71.7 us (39%)
  waiting for transfers between devices  55.9 us (31%)
  Pallas kernels  46.1 us (25%)
  local copies, waits for them, and re-layouts  5.57 us (3%)
  other arithmetic  2.26 us (1%)
    ppermute x31, starting transfers between devices, shift(): lax.ppermute(value, axis, [(i, (i + distance) % size) for i in range(size)])  45.2 us
    ppermute x31, waiting for transfers between devices, shift(): lax.ppermute(value, axis, [(i, (i + distance) % size) for i in range(size)])  43.1 us
    all_to_all x3, starting transfers between devices, exchange(): return lax.all_to_all(value, 'y', 0, 0, tiled=True)  17.6 us
    pallas_call x1, Pallas kernels, layer(): pl.pallas_call(functools.partial(attention_kernel, sizes=(y_size, z_size)...  13.1 us
    ppermute x4, waiting for transfers between devices, opposite(): return lax.ppermute(value, ('c', 'x'), pairs)  9.07 us
    pallas_call x1, Pallas kernels, layer(): pl.pallas_call(final_kernel, grid=(model // tile,), out_shape=array(rows,...  7.68 us
    pallas_call x1, Pallas kernels, layer(): pl.pallas_call(project_kernel, out_shape=[array(query_cap, heavy_width)]...  7.15 us
    pallas_call x1, Pallas kernels, layer(): pl.pallas_call(local_kernel, out_shape=[array(rows, width), array(rows, 2...  5.31 us
  transfers between devices with their start and end apart: 40, of which 13 were waited for; matrix products, arithmetic and copies ran while one was open for 2% of the time, Pallas kernels for 21%

commit v1 on v0

--- a/solution.py
+++ b/solution.py
@@ -317,16 +317,36 @@
         )
 
 
+def placed(slots_ref, source, rows, turn):
+    heads = 4
+    half = source.shape[0] // heads
+    parts = []
+    for position in range(heads):
+        head = (position + 2 * turn) % heads
+        start = head * half
+        packed = source[pl.ds(start if isinstance(turn, int) else pl.multiple_of(start, half), half), :]
+        parts.append(jnp.concatenate([packed[:, :HDIM], packed[:, HDIM:]], axis=0))
+    hot = hot_of(slots_ref[...], rows)
+    wide = jnp.concatenate(parts, axis=1)
+    return jnp.dot(hot, wide, preferred_element_type=jnp.float32).astype(jnp.bfloat16)
+
+
+def own_kernel(slots_ref, light_ref, light_out_ref, source_ref, own_ref, out_ref, mixed):
+    @pl.when(pl.program_id(0) == 0)
+    def _():
+        mixed[...] = placed(slots_ref, source_ref, light_ref.shape[0], 0)
+
+    acc = jnp.dot(light_ref[...], light_out_ref[...], preferred_element_type=jnp.float32)
+    out_ref[...] = acc + jnp.dot(mixed[...], own_ref[...], preferred_element_type=jnp.float32)
+
+
 def final_kernel(
     place_ref,
     slots_ref,
-    light_ref,
-    light_out_ref,
-    m0_ref,
+    sum_ref,
     m1_ref,
     m2_ref,
     m3_ref,
-    own_ref,
     near_ref,
     near2_ref,
     far_ref,
@@ -335,32 +355,17 @@
     mixed,
 ):
     pc = place_ref[2]
-    rows = light_ref.shape[0]
-    heads = 4
-    half = m0_ref.shape[0] // heads
 
     @pl.when(pl.program_id(0) == 0)
     def _():
-        slots = slots_ref.shape[1]
-        token = lax.broadcasted_iota(jnp.int32, (rows, slots), 0)
-        place = jnp.where(token == slots_ref[...], 1.0, 0.0).astype(jnp.bfloat16)
-        for number, source in enumerate((m0_ref, m1_ref, m2_ref, m3_ref)):
-            parts = []
-            for position in range(heads):
-                head = (position + 2 * pc) % heads if number == 3 else position
-                packed = source[pl.ds(pl.multiple_of(head * half, half), half), :]
-                parts.append(jnp.concatenate([packed[:, :HDIM], packed[:, HDIM:]], axis=0))
-            wide = jnp.concatenate(parts, axis=1)
-            mixed[number] = jnp.dot(place, wide, preferred_element_type=jnp.float32).astype(
-                jnp.bfloat16
-            )
-
-    acc = jnp.dot(light_ref[...], light_out_ref[...], preferred_element_type=jnp.float32)
-    acc += jnp.dot(mixed[0], own_ref[...], preferred_element_type=jnp.float32)
-    acc += jnp.dot(mixed[1 + pc], near_ref[...], preferred_element_type=jnp.float32)
-    acc += jnp.dot(mixed[2 - pc], near2_ref[...], preferred_element_type=jnp.float32)
+        for number, source in enumerate((m1_ref, m2_ref, m3_ref)):
+            mixed[number] = placed(slots_ref, source, sum_ref.shape[0], pc if number == 2 else 0)
+
+    acc = sum_ref[...]
+    acc += jnp.dot(mixed[pc], near_ref[...], preferred_element_type=jnp.float32)
+    acc += jnp.dot(mixed[1 - pc], near2_ref[...], preferred_element_type=jnp.float32)
     far = jnp.concatenate([far_ref[...], far2_ref[...]], axis=0)
-    acc += jnp.dot(mixed[3], far, preferred_element_type=jnp.float32)
+    acc += jnp.dot(mixed[2], far, preferred_element_type=jnp.float32)
     out_ref[...] = acc.astype(out_ref.dtype)
 
 
@@ -477,6 +482,10 @@
 
     ring = {0: column}
     for step in range(1, z_size // 2 + 1):
+        if step == 3:
+            ring[-2], key_starts, query_starts = lax.optimization_barrier(
+                (ring[-2], key_starts, query_starts)
+            )
         ring[-step] = shift(ring[-step + 1], "z", 1)
         if step < z_size // 2:
             ring[step] = shift(ring[step - 1], "z", -1)
@@ -510,27 +519,34 @@
     def columns(count):
         return pl.BlockSpec((count, tile), lambda j: (0, j))
 
+    so_far = pl.pallas_call(
+        own_kernel,
+        grid=(model // tile,),
+        out_shape=jax.ShapeDtypeStruct((rows, model), jnp.float32),
+        in_specs=[
+            whole(1, query_cap),
+            whole(rows, width),
+            columns(width),
+            whole(y_size * query_cap // 2, 2 * HDIM),
+            columns(heavy_width),
+        ],
+        out_specs=columns(rows),
+        scratch_shapes=[pltpu.VMEM((rows, heavy_width), bf16)],
+        cost_estimate=cost(2 * rows * 512 * model, 6 * rows * model),
+        name="combine_own",
+    )(query_slots, light_mixed, light_out, back, heavy_out)
     return pl.pallas_call(
         final_kernel,
         grid=(model // tile,),
         out_shape=array(rows, model),
-        in_specs=[smem(), whole(1, query_cap), whole(rows, width), columns(width)]
-        + [whole(y_size * query_cap // 2, 2 * HDIM)] * 4
-        + [columns(heavy_width)]
+        in_specs=[smem(), whole(1, query_cap), columns(rows)]
+        + [whole(y_size * query_cap // 2, 2 * HDIM)] * 3
         + [columns(p.shape[0]) for p in wo],
         out_specs=columns(rows),
-        scratch_shapes=[pltpu.VMEM((4, rows, heavy_width), bf16)],
-        cost_estimate=cost(2 * rows * 1280 * model, 10 * rows * model),
+        scratch_shapes=[pltpu.VMEM((3, rows, heavy_width), bf16)],
+        cost_estimate=cost(2 * rows * 768 * model, 10 * rows * model),
         name="combine",
-    )(
-        place,
-        query_slots,
-        light_mixed,
-        light_out,
-        *groups,
-        heavy_out,
-        *wo,
-    )
+    )(place, query_slots, so_far, *groups[1:], *wo)
 
 
 def solution(mesh):

time: 182 us -> 179 us (0.984)
  the two profiles are of different devices: /device:TPU:14 before, /device:TPU:36 now
where the time goes in v1:
time: 179 us; the launch traced here: 178 us
  starting transfers between devices  65.2 us (36%)
  Pallas kernels  57.3 us (32%)
  waiting for transfers between devices  47.2 us (26%)
  local copies, waits for them, and re-layouts  5.45 us (3%)
  other arithmetic  2.3 us (1%)
    ppermute x31, starting transfers between devices, shift(): lax.ppermute(value, axis, [(i, (i + distance) % size) for i in range(size)])  38.8 us
    ppermute x31, waiting for transfers between devices, shift(): lax.ppermute(value, axis, [(i, (i + distance) % size) for i in range(size)])  23.6 us
    pallas_call x1, Pallas kernels, layer(): pl.pallas_call(functools.partial(attention_kernel, sizes=(y_size, z_size)...  19.3 us
    all_to_all x3, waiting for transfers between devices, exchange(): return lax.all_to_all(value, 'y', 0, 0, tiled=True)  12.9 us
    all_to_all x3, starting transfers between devices, exchange(): return lax.all_to_all(value, 'y', 0, 0, tiled=True)  11.3 us
    ppermute x4, waiting for transfers between devices, opposite(): return lax.ppermute(value, ('c', 'x'), pairs)  10.1 us
    ppermute x4, starting transfers between devices, opposite(): return lax.ppermute(value, ('c', 'x'), pairs)  9.31 us
    pallas_call x1, Pallas kernels, layer(): pl.pallas_call(project_kernel, out_shape=[array(query_cap, heavy_width)]...  7.15 us
  transfers between devices with their start and end apart: 40, of which 12 were waited for; matrix products, arithmetic and copies ran while one was open for 2% of the time, Pallas kernels for 28%

profile of v1, /device:TPU:36, one launch (start us, length us, event | category | flops | bytes accessed | tf_op | source)
XLA Modules:
  0.0 177.8 jit_solution(12770777563078538356)
XLA Ops:
  1.8 3.3 %pick.1 = (bf16[48,2048]{1,0:T(8,128)(2,1)}, bf16[48,2048]{1,0:T(8,128)(2,1)}, bf16[48,2048]{1,0:T(8,128)(2,1)}, bf16[48,2048]{1,0:T(8,128)(2,1)}) custom-call(s32[6]{0:T(128)} %stack.27.place_ref, s32[64,128]{1,0:T(8,128)} %bitcast.26, bf16[512,2048]{1,0:T(8,128)(2,1)} %tokens_ref.5), custom_call_target="tpu_custom_call" | custom-call | flops 402653184 | bytes 2097152 | tf_op jit(solution)/shard_map/pick/pallas_call | solution.py:407
  7.2 2.0 %collective-permute-start.8 = (bf16[48,2048]{1,0:T(8,128)(2,1)}, bf16[48,2048]{1,0:T(8,128)(2,1)S(1)}, u32[]{:S(2)}, u32[]{:S(2)}) collective-permute-start(bf16[48,2048]{1,0:T(8,128)(2,1)} %get-tuple-element.29), channel_id=1, source_target_pairs={{0,2},{1,3},{2,0},{3,1},{4,6},{5,7},{6,4},{7,5},{8,10},{9,11},{10,... | collective-permute-start | bytes 589832 | tf_op jit(solution)/shard_map/ppermute | solution.py:24
  9.2 10.1 %collective-permute-done.near_ref = bf16[2048,256]{1,0:T(8,128)(2,1)} collective-permute-done((bf16[2048,256]{1,0:T(8,128)(2,1)}, bf16[2048,256]{1,0:T(8,128)(2,1)}, u32[]{:S(2)}, u32[]{:S(2)}) %collective-permute-start) | collective-permute-done | bytes 1048608 | tf_op jit(solution)/shard_map/ppermute | solution.py:31
  24.5 2.8 %collective-permute-start.10 = (bf16[48,2048]{1,0:T(8,128)(2,1)S(1)}, bf16[48,2048]{1,0:T(8,128)(2,1)S(1)}, u32[]{:S(2)}, u32[]{:S(2)}) collective-permute-start(bf16[48,2048]{1,0:T(8,128)(2,1)S(1)} %add_add_fusion.own_ref), channel_id=1, source_target_pairs={{0,2},{1,3},{2,0},{3,1},{4,6},{5,7},{6,4},{7,5},{8,10},{9,11},{10,... | collective-permute-start | bytes 589832 | tf_op jit(solution)/shard_map/ppermute | solution.py:24
  27.3 2.5 %collective-permute-start.9 = (bf16[48,2048]{1,0:T(8,128)(2,1)S(1)}, bf16[48,2048]{1,0:T(8,128)(2,1)S(1)}, u32[]{:S(2)}, u32[]{:S(2)}) collective-permute-start(bf16[48,2048]{1,0:T(8,128)(2,1)S(1)} %add_add_fusion.own_ref), channel_id=1, source_target_pairs={{0,1},{1,2},{2,3},{3,0},{4,5},{5,6},{6,7},{7,4},{8,9},{9,10},{10,1... | collective-permute-start | bytes 589832 | tf_op jit(solution)/shard_map/ppermute | solution.py:24
  29.8 2.4 %collective-permute-done.11.c_ref = bf16[48,2048]{1,0:T(8,128)(2,1)S(1)} collective-permute-done((bf16[48,2048]{1,0:T(8,128)(2,1)S(1)}, bf16[48,2048]{1,0:T(8,128)(2,1)S(1)}, u32[]{:S(2)}, u32[]{:S(2)}) %collective-permute-start.11) | collective-permute-done | bytes 196640 | tf_op jit(solution)/shard_map/ppermute | solution.py:24
  32.3 6.1 %collective-permute-start.33 = (bf16[256,2048]{1,0:T(8,128)(2,1)S(1)}, bf16[256,2048]{1,0:T(8,128)(2,1)S(1)}, u32[]{:S(2)}, u32[]{:S(2)}) collective-permute-start(bf16[256,2048]{1,0:T(8,128)(2,1)S(1)} %copy-done.1), channel_id=1, source_target_pairs={{0,1},{1,2},{2,3},{3,0},{4,7},{5,4},{6,5},{7,6},{8,9},{9,10},{10,1... | collective-permute-start | bytes 3145736 | tf_op jit(solution)/shard_map/ppermute | solution.py:31
  39.7 3.3 %key_value_heads.1 = bf16[768,128]{1,0:T(8,128)(2,1)} custom-call(s32[6]{0:T(128)} %stack.27.place_ref, bf16[48,2048]{1,0:T(8,128)(2,1)} %copy-done.4, bf16[48,2048]{1,0:T(8,128)(2,1)} %copy-done.12, bf16[48,2048]{1,0:T(8,128)(2,1)} %copy-done.11, bf16[48,2048]{1,0:T(8,128)(2,1)} %copy-done.10, bf16[2048,256]{1,0:T(8,128)(2,1)} %key_ref.3, ...), custom_call_target="tpu_custom_call" | custom-call | flops 402653184 | bytes 2097152 | tf_op jit(solution)/shard_map/key_value_heads/pallas_call | solution.py:446
  43.0 4.5 %all-to-all-start = ((bf16[4,192,128]{2,1,0:T(8,128)(2,1)}), bf16[4,192,128]{2,1,0:T(8,128)(2,1)S(1)}, u32[]{:S(2)}, u32[]{:S(2)}) async-start(bf16[4,192,128]{2,1,0:T(8,128)(2,1)} %bitcast.19), calls=%async_computation | async-start | bytes 393216 | tf_op jit(solution)/shard_map/all_to_all | solution.py:213
  47.4 6.3 %all-to-all-done = bf16[4,192,128]{2,1,0:T(8,128)(2,1)S(1)} async-done(((bf16[4,192,128]{2,1,0:T(8,128)(2,1)}), bf16[4,192,128]{2,1,0:T(8,128)(2,1)S(1)}, u32[]{:S(2)}, u32[]{:S(2)}) %all-to-all-start) | async-done | bytes 196640 | tf_op jit(solution)/shard_map/all_to_all | solution.py:213
  55.8 4.4 %collective-permute-done.12.refs_2_ = bf16[768,128]{1,0:T(8,128)(2,1)S(1)} collective-permute-done((bf16[768,128]{1,0:T(8,128)(2,1)S(1)}, bf16[768,128]{1,0:T(8,128)(2,1)S(1)}, u32[]{:S(2)}, u32[]{:S(2)}) %collective-permute-start.12) | collective-permute-done | bytes 196640 | tf_op jit(solution)/shard_map/ppermute | solution.py:24
  60.2 2.5 %collective-permute-start.13 = (bf16[768,128]{1,0:T(8,128)(2,1)S(1)}, bf16[768,128]{1,0:T(8,128)(2,1)}, u32[]{:S(2)}, u32[]{:S(2)}) collective-permute-start(bf16[768,128]{1,0:T(8,128)(2,1)S(1)} %collective-permute-done.12.refs_2_), channel_id=1, source_target_pairs={{0,8},{8,16},{16,24},{24,32},{32,40},{40,48},{48,56},{56,0},{1,9},... | collective-permute-start | bytes 589832 | tf_op jit(solution)/shard_map/ppermute | solution.py:24
  64.0 3.1 %collective-permute-done.13.refs_4_ = bf16[768,128]{1,0:T(8,128)(2,1)} collective-permute-done((bf16[768,128]{1,0:T(8,128)(2,1)S(1)}, bf16[768,128]{1,0:T(8,128)(2,1)}, u32[]{:S(2)}, u32[]{:S(2)}) %collective-permute-start.13) | collective-permute-done | bytes 196640 | tf_op jit(solution)/shard_map/ppermute | solution.py:24
  67.1 3.4 %collective-permute-start.18 = (bf16[768,128]{1,0:T(8,128)(2,1)S(1)}, bf16[768,128]{1,0:T(8,128)(2,1)}, u32[]{:S(2)}, u32[]{:S(2)}) collective-permute-start(bf16[768,128]{1,0:T(8,128)(2,1)S(1)} %collective-permute-done.17.refs_3_), channel_id=1, source_target_pairs={{0,56},{8,0},{16,8},{24,16},{32,24},{40,32},{48,40},{56,48},{1,57}... | collective-permute-start | bytes 589832 | tf_op jit(solution)/shard_map/ppermute | solution.py:24
  70.6 7.2 %query_project.1 = (bf16[512,256]{1,0:T(8,128)(2,1)}, bf16[512,256]{1,0:T(8,128)(2,1)}, bf16[512,256]{1,0:T(8,128)(2,1)}, bf16[512,256]{1,0:T(8,128)(2,1)}, s32[1,512]{1,0:T(1,128)}) custom-call(s32[6]{0:T(128)} %stack.27.place_ref, s32[64,128]{1,0:T(8,128)} %bitcast.27, bf16[512,2048]{1,0:T(8,128)(2,1)} %tokens_ref.5, bf16[2048,256]{1,0:T(8,128)(2,1)} %own_ref.2, ...), custom_call_target="tpu_custom_call" | custom-call | flops 2147483648 | bytes 4194304 | tf_op jit(solution)/shard_map/query_project/pallas_call | solution.py:457
  79.9 3.1 %collective-permute-start.16 = (bf16[512,256]{1,0:T(8,128)(2,1)}, bf16[512,256]{1,0:T(8,128)(2,1)S(1)}, u32[]{:S(2)}, u32[]{:S(2)}) collective-permute-start(bf16[512,256]{1,0:T(8,128)(2,1)} %get-tuple-element.35), channel_id=1, source_target_pairs={{0,2},{1,3},{2,0},{3,1},{4,6},{5,7},{6,4},{7,5},{8,10},{9,11},{10,... | collective-permute-start | bytes 786440 | tf_op jit(solution)/shard_map/ppermute | solution.py:24
  83.8 3.4 %collective-permute-done.14.a_ref = bf16[512,256]{1,0:T(8,128)(2,1)S(1)} collective-permute-done((bf16[512,256]{1,0:T(8,128)(2,1)}, bf16[512,256]{1,0:T(8,128)(2,1)S(1)}, u32[]{:S(2)}, u32[]{:S(2)}) %collective-permute-start.14) | collective-permute-done | bytes 262176 | tf_op jit(solution)/shard_map/ppermute | solution.py:24
  90.1 4.8 %collective-permute-done.16.c_ref = bf16[512,256]{1,0:T(8,128)(2,1)S(1)} collective-permute-done((bf16[512,256]{1,0:T(8,128)(2,1)}, bf16[512,256]{1,0:T(8,128)(2,1)S(1)}, u32[]{:S(2)}, u32[]{:S(2)}) %collective-permute-start.16) | collective-permute-done | bytes 262176 | tf_op jit(solution)/shard_map/ppermute | solution.py:24
  95.7 2.1 %query_heads.1 = bf16[1024,128]{1,0:T(8,128)(2,1)} custom-call(bf16[512,256]{1,0:T(8,128)(2,1)} %get-tuple-element.32.own_ref, bf16[512,256]{1,0:T(8,128)(2,1)} %copy-done.7, bf16[512,256]{1,0:T(8,128)(2,1)} %collective-permute-done.15.b_ref, bf16[512,256]{1,0:T(8,128)(2,1)} %copy-done.8), custom_call_target="tpu_custom_call" | custom-call | flops 524288 | bytes 1310720 | tf_op jit(solution)/shard_map/query_heads/pallas_call | solution.py:471
  98.3 2.7 %collective-permute-done.21.refs_8_ = bf16[768,128]{1,0:T(8,128)(2,1)} collective-permute-done((bf16[768,128]{1,0:T(8,128)(2,1)}, bf16[768,128]{1,0:T(8,128)(2,1)}, u32[]{:S(2)}, u32[]{:S(2)}) %collective-permute-start.21) | collective-permute-done | bytes 196640 | tf_op jit(solution)/shard_map/ppermute | solution.py:24
  101.0 3.4 %all-to-all-start.1 = ((bf16[4,256,128]{2,1,0:T(8,128)(2,1)}), bf16[4,256,128]{2,1,0:T(8,128)(2,1)S(1)}, u32[]{:S(2)}, u32[]{:S(2)}) async-start(bf16[4,256,128]{2,1,0:T(8,128)(2,1)} %bitcast.18), calls=%async_computation.1 | async-start | bytes 524288 | tf_op jit(solution)/shard_map/all_to_all | solution.py:213
  105.4 6.6 %all-to-all-done.1 = bf16[4,256,128]{2,1,0:T(8,128)(2,1)S(1)} async-done(((bf16[4,256,128]{2,1,0:T(8,128)(2,1)}), bf16[4,256,128]{2,1,0:T(8,128)(2,1)S(1)}, u32[]{:S(2)}, u32[]{:S(2)}) %all-to-all-start.1) | async-done | bytes 262176 | tf_op jit(solution)/shard_map/all_to_all | solution.py:213
  112.7 19.3 %heavy_attention.1 = bf16[1024,128]{1,0:T(8,128)(2,1)} custom-call(s32[6]{0:T(128)} %stack.27.place_ref, s32[65]{0:T(128)} %get-tuple-element.30.query_starts_ref, s32[65]{0:T(128)} %get-tuple-element.31.key_starts_ref, bf16[1024,128]{1,0:T(8,128)(2,1)} %bitcast.20, bf16[768,128]{1,0:T(8,128)(2,1)} %bitcast.25, bf16[768,128]{1,0:T(8,128)(2,1)} %copy-done.17, ...), custom_call_target="tpu_custom_call" | custom-call | flops 12884901888 | bytes 3145728 | tf_op jit(solution)/shard_map/heavy_attention/pallas_call | solution.py:497
  132.0 3.4 %all-to-all-start.2 = ((bf16[4,256,128]{2,1,0:T(8,128)(2,1)}), bf16[4,256,128]{2,1,0:T(8,128)(2,1)S(1)}, u32[]{:S(2)}, u32[]{:S(2)}) async-start(bf16[4,256,128]{2,1,0:T(8,128)(2,1)} %bitcast.21), calls=%async_computation.2 | async-start | bytes 524288 | tf_op jit(solution)/shard_map/all_to_all | solution.py:213
  135.4 5.3 %light_project.1 = (bf16[512,256]{1,0:T(8,128)(2,1)}, bf16[512,512]{1,0:T(8,128)(2,1)}, bf16[128,512]{1,0:T(8,128)(2,1)}, bf16[128,512]{1,0:T(8,128)(2,1)}) custom-call(bf16[512,2048]{1,0:T(8,128)(2,1)} %tokens_ref.5, bf16[2048,256]{1,0:T(8,128)(2,1)} %query_ref.1, bf16[2048,256]{1,0:T(8,128)(2,1)} %key_ref.2, bf16[2048,256]{1,0:T(8,128)(2,1)} %value_ref.2), custom_call_target="tpu_custom_call" | custom-call | flops 1610612736 | bytes 5242880 | tf_op jit(solution)/shard_map/light_project/pallas_call | solution.py:420
  140.8 3.5 %collective-permute-start.4 = (bf16[128,512]{1,0:T(8,128)(2,1)}, bf16[128,512]{1,0:T(8,128)(2,1)S(1)}, u32[]{:S(2)}, u32[]{:S(2)}) collective-permute-start(bf16[128,512]{1,0:T(8,128)(2,1)} %get-tuple-element.23), channel_id=1, source_target_pairs={{0,1},{1,2},{2,3},{3,4},{4,5},{5,6},{6,7},{7,8},{8,9},{9,10},{10,1... | collective-permute-start | bytes 393224 | tf_op jit(solution)/shard_map/ppermute | solution.py:430
  144.2 2.4 %collective-permute-start.5 = (bf16[128,512]{1,0:T(8,128)(2,1)}, bf16[128,512]{1,0:T(8,128)(2,1)}, u32[]{:S(2)}, u32[]{:S(2)}) collective-permute-start(bf16[128,512]{1,0:T(8,128)(2,1)} %get-tuple-element.25), channel_id=1, source_target_pairs={{1,0},{2,1},{3,2},{4,3},{5,4},{6,5},{7,6},{8,7},{9,8},{10,9},{11,1... | collective-permute-start | bytes 393224 | tf_op jit(solution)/shard_map/ppermute | solution.py:431
  146.6 5.1 %collective-permute-start.32 = (bf16[1024,128]{1,0:T(8,128)(2,1)S(1)}, bf16[1024,128]{1,0:T(8,128)(2,1)}, u32[]{:S(2)}, u32[]{:S(2)}) collective-permute-start(bf16[1024,128]{1,0:T(8,128)(2,1)S(1)} %bitcast.14), channel_id=1, source_target_pairs={{0,2},{1,3},{2,0},{3,1},{4,6},{5,7},{6,4},{7,5},{8,10},{9,11},{10,... | collective-permute-start | bytes 786440 | tf_op jit(solution)/shard_map/ppermute | solution.py:24
  152.3 7.4 %collective-permute-start.30 = (bf16[1024,128]{1,0:T(8,128)(2,1)S(1)}, bf16[1024,128]{1,0:T(8,128)(2,1)}, u32[]{:S(2)}, u32[]{:S(2)}) collective-permute-start(bf16[1024,128]{1,0:T(8,128)(2,1)S(1)} %bitcast.16), channel_id=1, source_target_pairs={{0,1},{1,2},{2,3},{3,0},{4,5},{5,6},{6,7},{7,4},{8,9},{9,10},{10,1... | collective-permute-start | bytes 786440 | tf_op jit(solution)/shard_map/ppermute | solution.py:24
  159.7 4.2 %light.1.light_ref = bf16[512,256]{1,0:T(8,128)(2,1)} custom-call(s32[1]{0:T(128)} %bitcast.5.first_ref, bf16[512,256]{1,0:T(8,128)(2,1)} %get-tuple-element.22.q_ref, bf16[128,512]{1,0:T(8,128)(2,1)} %copy-done.21, bf16[512,512]{1,0:T(8,128)(2,1)} %get-tuple-element.24.own_ref, bf16[128,512]{1,0:T(8,128)(2,1)} %collective-permute-done.5.next_ref), custom_call_target="tpu_custom_call" | custom-call | flops 1073741824 | bytes 1048576 | tf_op jit(solution)/shard_map/light/pallas_call | solution.py:432
  164.0 5.6 %combine_own.1.sum_ref = f32[512,2048]{1,0:T(8,128)} custom-call(s32[1,512]{1,0:T(1,128)} %get-tuple-element.21.slots_ref, bf16[512,256]{1,0:T(8,128)(2,1)} %light.1.light_ref, bf16[256,2048]{1,0:T(8,128)(2,1)} %light_out_ref.1, bf16[1024,128]{1,0:T(8,128)(2,1)} %bitcast.17, bf16[256,2048]{1,0:T(8,128)(2,1)} %own_ref.3), custom_call_target="tpu_custom_call" | custom-call | flops 1073741824 | bytes 6291456 | tf_op jit(solution)/shard_map/combine_own/pallas_call | solution.py:522
  170.8 7.1 %combine.1 = bf16[512,2048]{1,0:T(8,128)(2,1)} custom-call(s32[6]{0:T(128)} %stack.27.place_ref, s32[1,512]{1,0:T(1,128)} %get-tuple-element.21.slots_ref, f32[512,2048]{1,0:T(8,128)} %combine_own.1.sum_ref, bf16[1024,128]{1,0:T(8,128)(2,1)} %collective-permute-done.30.m1_ref, bf16[1024,128]{1,0:T(8,128)(2,1)} %collective-permute-done.31.m2_ref, ...), custom_call_target="tpu_custom_call" | custom-call | flops 1610612736 | bytes 10485760 | tf_op jit(solution)/shard_map/combine/pallas_call | solution.py:538
  (107 shorter events, 24.2 us)
Async XLA Ops:
  0.0 19.3 %collective-permute-start = (bf16[2048,256]{1,0:T(8,128)(2,1)}, bf16[2048,256]{1,0:T(8,128)(2,1)}, u32[]{:S(2)}, u32[]{:S(2)}) collective-permute-start(bf16[2048,256]{1,0:T(8,128)(2,1)} %own_ref.2), channel_id=1, source_target_pairs={{0,1},{1,2},{2,3},{3,0},{4,7},{5,4},{6,5},{7,6},{8,9},{9,10},{10,1... | collective-permute-start | bytes 3145736 | tf_op jit(solution)/shard_map/ppermute | solution.py:31
  5.2 16.5 %collective-permute-start.6 = (bf16[48,2048]{1,0:T(8,128)(2,1)}, bf16[48,2048]{1,0:T(8,128)(2,1)S(1)}, u32[]{:S(2)}, u32[]{:S(2)}) collective-permute-start(bf16[48,2048]{1,0:T(8,128)(2,1)} %get-tuple-element.27), channel_id=1, source_target_pairs={{0,1},{1,2},{2,3},{3,0},{4,5},{5,6},{6,7},{7,4},{8,9},{9,10},{10,1... | collective-permute-start | bytes 589832 | tf_op jit(solution)/shard_map/ppermute | solution.py:24
  5.6 16.1 %collective-permute-start.7 = (bf16[48,2048]{1,0:T(8,128)(2,1)}, bf16[48,2048]{1,0:T(8,128)(2,1)S(1)}, u32[]{:S(2)}, u32[]{:S(2)}) collective-permute-start(bf16[48,2048]{1,0:T(8,128)(2,1)} %get-tuple-element.28), channel_id=1, source_target_pairs={{0,3},{1,0},{2,1},{3,2},{4,7},{5,4},{6,5},{7,6},{8,11},{9,8},{10,9... | collective-permute-start | bytes 589832 | tf_op jit(solution)/shard_map/ppermute | solution.py:24
  7.2 16.2 %collective-permute-start.8 = (bf16[48,2048]{1,0:T(8,128)(2,1)}, bf16[48,2048]{1,0:T(8,128)(2,1)S(1)}, u32[]{:S(2)}, u32[]{:S(2)}) collective-permute-start(bf16[48,2048]{1,0:T(8,128)(2,1)} %get-tuple-element.29), channel_id=1, source_target_pairs={{0,2},{1,3},{2,0},{3,1},{4,6},{5,7},{6,4},{7,5},{8,10},{9,11},{10,... | collective-permute-start | bytes 589832 | tf_op jit(solution)/shard_map/ppermute | solution.py:24
  20.4 27.0 %collective-permute-start.2 = (bf16[1024,256]{1,0:T(8,128)(2,1)S(1)}, bf16[1024,256]{1,0:T(8,128)(2,1)}, u32[]{:S(2)}, u32[]{:S(2)}) collective-permute-start(bf16[1024,256]{1,0:T(8,128)(2,1)S(1)} %constant_dynamic-slice_fusion.1), channel_id=1, source_target_pairs={{0,1},{1,2},{2,3},{3,0},{4,7},{5,4},{6,5},{7,6},{8,9},{9,10},{10,1... | collective-permute-start | bytes 1572872 | tf_op jit(solution)/shard_map/ppermute | solution.py:31
  21.7 48.9 %collective-permute-start.1 = (bf16[2048,256]{1,0:T(8,128)(2,1)}, bf16[2048,256]{1,0:T(8,128)(2,1)}, u32[]{:S(2)}, u32[]{:S(2)}) collective-permute-start(bf16[2048,256]{1,0:T(8,128)(2,1)} %collective-permute-done.near_ref), channel_id=1, source_target_pairs={{0,4},{4,0},{1,5},{5,1},{2,6},{6,2},{3,7},{7,3},{8,12},{12,8},{9,1... | collective-permute-start | bytes 3145736 | tf_op jit(solution)/shard_map/ppermute | solution.py:24
  24.5 13.8 %collective-permute-start.10 = (bf16[48,2048]{1,0:T(8,128)(2,1)S(1)}, bf16[48,2048]{1,0:T(8,128)(2,1)S(1)}, u32[]{:S(2)}, u32[]{:S(2)}) collective-permute-start(bf16[48,2048]{1,0:T(8,128)(2,1)S(1)} %add_add_fusion.own_ref), channel_id=1, source_target_pairs={{0,2},{1,3},{2,0},{3,1},{4,6},{5,7},{6,4},{7,5},{8,10},{9,11},{10,... | collective-permute-start | bytes 589832 | tf_op jit(solution)/shard_map/ppermute | solution.py:24
  27.3 11.0 %collective-permute-start.9 = (bf16[48,2048]{1,0:T(8,128)(2,1)S(1)}, bf16[48,2048]{1,0:T(8,128)(2,1)S(1)}, u32[]{:S(2)}, u32[]{:S(2)}) collective-permute-start(bf16[48,2048]{1,0:T(8,128)(2,1)S(1)} %add_add_fusion.own_ref), channel_id=1, source_target_pairs={{0,1},{1,2},{2,3},{3,0},{4,5},{5,6},{6,7},{7,4},{8,9},{9,10},{10,1... | collective-permute-start | bytes 589832 | tf_op jit(solution)/shard_map/ppermute | solution.py:24
  32.3 47.6 %collective-permute-start.33 = (bf16[256,2048]{1,0:T(8,128)(2,1)S(1)}, bf16[256,2048]{1,0:T(8,128)(2,1)S(1)}, u32[]{:S(2)}, u32[]{:S(2)}) collective-permute-start(bf16[256,2048]{1,0:T(8,128)(2,1)S(1)} %copy-done.1), channel_id=1, source_target_pairs={{0,1},{1,2},{2,3},{3,0},{4,7},{5,4},{6,5},{7,6},{8,9},{9,10},{10,1... | collective-permute-start | bytes 3145736 | tf_op jit(solution)/shard_map/ppermute | solution.py:31
  43.0 10.8 %all-to-all-start = ((bf16[4,192,128]{2,1,0:T(8,128)(2,1)}), bf16[4,192,128]{2,1,0:T(8,128)(2,1)S(1)}, u32[]{:S(2)}, u32[]{:S(2)}) async-start(bf16[4,192,128]{2,1,0:T(8,128)(2,1)} %bitcast.19), calls=%async_computation | async-start | bytes 393216 | tf_op jit(solution)/shard_map/all_to_all | solution.py:213
  47.4 19.7 %collective-permute-start.3 = (bf16[1024,256]{1,0:T(8,128)(2,1)}, bf16[1024,256]{1,0:T(8,128)(2,1)S(1)}, u32[]{:S(2)}, u32[]{:S(2)}) collective-permute-start(bf16[1024,256]{1,0:T(8,128)(2,1)} %collective-permute-done.2.far_ref), channel_id=1, source_target_pairs={{0,4},{4,0},{1,5},{5,1},{2,6},{6,2},{3,7},{7,3},{8,12},{12,8},{9,1... | collective-permute-start | bytes 1572872 | tf_op jit(solution)/shard_map/ppermute | solution.py:24
  55.7 8.3 %collective-permute-start.17 = (bf16[768,128]{1,0:T(8,128)(2,1)S(1)}, bf16[768,128]{1,0:T(8,128)(2,1)S(1)}, u32[]{:S(2)}, u32[]{:S(2)}) collective-permute-start(bf16[768,128]{1,0:T(8,128)(2,1)S(1)} %bitcast.23), channel_id=1, source_target_pairs={{0,56},{8,0},{16,8},{24,16},{32,24},{40,32},{48,40},{56,48},{1,57}... | collective-permute-start | bytes 589832 | tf_op jit(solution)/shard_map/ppermute | solution.py:24
  64.0 13.7 %collective-permute-start.22 = (bf16[768,128]{1,0:T(8,128)(2,1)S(1)}, bf16[768,128]{1,0:T(8,128)(2,1)S(1)}, u32[]{:S(2)}, u32[]{:S(2)}) collective-permute-start(bf16[768,128]{1,0:T(8,128)(2,1)S(1)} %bitcast.24), channel_id=1, source_target_pairs={{0,4},{4,0},{1,5},{5,1},{2,6},{6,2},{3,7},{7,3},{8,12},{12,8},{9,1... | collective-permute-start | bytes 589832 | tf_op jit(solution)/shard_map/ppermute | solution.py:24
  67.1 10.7 %collective-permute-start.24 = (bf16[768,128]{1,0:T(8,128)(2,1)S(1)}, bf16[768,128]{1,0:T(8,128)(2,1)}, u32[]{:S(2)}, u32[]{:S(2)}) collective-permute-start(bf16[768,128]{1,0:T(8,128)(2,1)S(1)} %collective-permute-done.17.refs_3_), channel_id=1, source_target_pairs={{0,4},{4,0},{1,5},{5,1},{2,6},{6,2},{3,7},{7,3},{8,12},{12,8},{9,1... | collective-permute-start | bytes 589832 | tf_op jit(solution)/shard_map/ppermute | solution.py:24
  67.1 15.9 %collective-permute-start.18 = (bf16[768,128]{1,0:T(8,128)(2,1)S(1)}, bf16[768,128]{1,0:T(8,128)(2,1)}, u32[]{:S(2)}, u32[]{:S(2)}) collective-permute-start(bf16[768,128]{1,0:T(8,128)(2,1)S(1)} %collective-permute-done.17.refs_3_), channel_id=1, source_target_pairs={{0,56},{8,0},{16,8},{24,16},{32,24},{40,32},{48,40},{56,48},{1,57}... | collective-permute-start | bytes 589832 | tf_op jit(solution)/shard_map/ppermute | solution.py:24
  70.6 13.2 %collective-permute-start.19 = (bf16[768,128]{1,0:T(8,128)(2,1)}, bf16[768,128]{1,0:T(8,128)(2,1)}, u32[]{:S(2)}, u32[]{:S(2)}) collective-permute-start(bf16[768,128]{1,0:T(8,128)(2,1)} %collective-permute-done.13.refs_4_), channel_id=1, source_target_pairs={{0,8},{8,16},{16,24},{24,32},{32,40},{40,48},{48,56},{56,0},{1,9},... | collective-permute-start | bytes 589832 | tf_op jit(solution)/shard_map/ppermute | solution.py:24
  77.7 9.5 %collective-permute-start.14 = (bf16[512,256]{1,0:T(8,128)(2,1)}, bf16[512,256]{1,0:T(8,128)(2,1)S(1)}, u32[]{:S(2)}, u32[]{:S(2)}) collective-permute-start(bf16[512,256]{1,0:T(8,128)(2,1)} %get-tuple-element.33), channel_id=1, source_target_pairs={{0,3},{1,0},{2,1},{3,2},{4,7},{5,4},{6,5},{7,6},{8,11},{9,8},{10,9... | collective-permute-start | bytes 786440 | tf_op jit(solution)/shard_map/ppermute | solution.py:24
  77.8 10.3 %collective-permute-start.15 = (bf16[512,256]{1,0:T(8,128)(2,1)}, bf16[512,256]{1,0:T(8,128)(2,1)}, u32[]{:S(2)}, u32[]{:S(2)}) collective-permute-start(bf16[512,256]{1,0:T(8,128)(2,1)} %get-tuple-element.34), channel_id=1, source_target_pairs={{0,1},{1,2},{2,3},{3,0},{4,5},{5,6},{6,7},{7,4},{8,9},{9,10},{10,1... | collective-permute-start | bytes 786440 | tf_op jit(solution)/shard_map/ppermute | solution.py:24
  79.9 15.1 %collective-permute-start.16 = (bf16[512,256]{1,0:T(8,128)(2,1)}, bf16[512,256]{1,0:T(8,128)(2,1)S(1)}, u32[]{:S(2)}, u32[]{:S(2)}) collective-permute-start(bf16[512,256]{1,0:T(8,128)(2,1)} %get-tuple-element.35), channel_id=1, source_target_pairs={{0,2},{1,3},{2,0},{3,1},{4,6},{5,7},{6,4},{7,5},{8,10},{9,11},{10,... | collective-permute-start | bytes 786440 | tf_op jit(solution)/shard_map/ppermute | solution.py:24
  83.0 22.3 %collective-permute-start.35 = (bf16[128,2048]{1,0:T(8,128)(2,1)S(1)}, bf16[128,2048]{1,0:T(8,128)(2,1)S(1)}, u32[]{:S(2)}, u32[]{:S(2)}) collective-permute-start(bf16[128,2048]{1,0:T(8,128)(2,1)S(1)} %constant_dynamic-slice_fusion), channel_id=1, source_target_pairs={{0,1},{1,2},{2,3},{3,0},{4,7},{5,4},{6,5},{7,6},{8,9},{9,10},{10,1... | collective-permute-start | bytes 1572872 | tf_op jit(solution)/shard_map/ppermute | solution.py:31
  83.8 13.9 %collective-permute-start.23 = (bf16[768,128]{1,0:T(8,128)(2,1)S(1)}, bf16[768,128]{1,0:T(8,128)(2,1)S(1)}, u32[]{:S(2)}, u32[]{:S(2)}) collective-permute-start(bf16[768,128]{1,0:T(8,128)(2,1)S(1)} %collective-permute-done.12.refs_2_), channel_id=1, source_target_pairs={{0,4},{4,0},{1,5},{5,1},{2,6},{6,2},{3,7},{7,3},{8,12},{12,8},{9,1... | collective-permute-start | bytes 589832 | tf_op jit(solution)/shard_map/ppermute | solution.py:24
  87.2 10.5 %collective-permute-start.26 = (bf16[768,128]{1,0:T(8,128)(2,1)}, bf16[768,128]{1,0:T(8,128)(2,1)}, u32[]{:S(2)}, u32[]{:S(2)}) collective-permute-start(bf16[768,128]{1,0:T(8,128)(2,1)} %collective-permute-done.18.refs_5_), channel_id=1, source_target_pairs={{0,4},{4,0},{1,5},{5,1},{2,6},{6,2},{3,7},{7,3},{8,12},{12,8},{9,1... | collective-permute-start | bytes 589832 | tf_op jit(solution)/shard_map/ppermute | solution.py:24
  88.2 10.1 %collective-permute-start.20 = (bf16[768,128]{1,0:T(8,128)(2,1)}, bf16[768,128]{1,0:T(8,128)(2,1)}, u32[]{:S(2)}, u32[]{:S(2)}) collective-permute-start(bf16[768,128]{1,0:T(8,128)(2,1)} %collective-permute-done.18.refs_5_), channel_id=1, source_target_pairs={{0,56},{8,0},{16,8},{24,16},{32,24},{40,32},{48,40},{56,48},{1,57}... | collective-permute-start | bytes 589832 | tf_op jit(solution)/shard_map/ppermute | solution.py:24
  101.0 11.0 %all-to-all-start.1 = ((bf16[4,256,128]{2,1,0:T(8,128)(2,1)}), bf16[4,256,128]{2,1,0:T(8,128)(2,1)S(1)}, u32[]{:S(2)}, u32[]{:S(2)}) async-start(bf16[4,256,128]{2,1,0:T(8,128)(2,1)} %bitcast.18), calls=%async_computation.1 | async-start | bytes 524288 | tf_op jit(solution)/shard_map/all_to_all | solution.py:213
  104.5 65.1 %collective-permute-start.34 = (bf16[256,2048]{1,0:T(8,128)(2,1)S(1)}, bf16[256,2048]{1,0:T(8,128)(2,1)S(1)}, u32[]{:S(2)}, u32[]{:S(2)}) collective-permute-start(bf16[256,2048]{1,0:T(8,128)(2,1)S(1)} %collective-permute-done.33.near_ref), channel_id=1, source_target_pairs={{0,4},{4,0},{1,5},{5,1},{2,6},{6,2},{3,7},{7,3},{8,12},{12,8},{9,1... | collective-permute-start | bytes 3145736 | tf_op jit(solution)/shard_map/ppermute | solution.py:24
  105.3 64.3 %collective-permute-start.36 = (bf16[128,2048]{1,0:T(8,128)(2,1)S(1)}, bf16[128,2048]{1,0:T(8,128)(2,1)S(1)}, u32[]{:S(2)}, u32[]{:S(2)}) collective-permute-start(bf16[128,2048]{1,0:T(8,128)(2,1)S(1)} %collective-permute-done.35.far_ref), channel_id=1, source_target_pairs={{0,4},{4,0},{1,5},{5,1},{2,6},{6,2},{3,7},{7,3},{8,12},{12,8},{9,1... | collective-permute-start | bytes 1572872 | tf_op jit(solution)/shard_map/ppermute | solution.py:24
  132.0 14.6 %all-to-all-start.2 = ((bf16[4,256,128]{2,1,0:T(8,128)(2,1)}), bf16[4,256,128]{2,1,0:T(8,128)(2,1)S(1)}, u32[]{:S(2)}, u32[]{:S(2)}) async-start(bf16[4,256,128]{2,1,0:T(8,128)(2,1)} %bitcast.21), calls=%async_computation.2 | async-start | bytes 524288 | tf_op jit(solution)/shard_map/all_to_all | solution.py:213
  140.8 11.0 %collective-permute-start.4 = (bf16[128,512]{1,0:T(8,128)(2,1)}, bf16[128,512]{1,0:T(8,128)(2,1)S(1)}, u32[]{:S(2)}, u32[]{:S(2)}) collective-permute-start(bf16[128,512]{1,0:T(8,128)(2,1)} %get-tuple-element.23), channel_id=1, source_target_pairs={{0,1},{1,2},{2,3},{3,4},{4,5},{5,6},{6,7},{7,8},{8,9},{9,10},{10,1... | collective-permute-start | bytes 393224 | tf_op jit(solution)/shard_map/ppermute | solution.py:430
  144.2 8.1 %collective-permute-start.5 = (bf16[128,512]{1,0:T(8,128)(2,1)}, bf16[128,512]{1,0:T(8,128)(2,1)}, u32[]{:S(2)}, u32[]{:S(2)}) collective-permute-start(bf16[128,512]{1,0:T(8,128)(2,1)} %get-tuple-element.25), channel_id=1, source_target_pairs={{1,0},{2,1},{3,2},{4,3},{5,4},{6,5},{7,6},{8,7},{9,8},{10,9},{11,1... | collective-permute-start | bytes 393224 | tf_op jit(solution)/shard_map/ppermute | solution.py:431
  146.6 23.0 %collective-permute-start.32 = (bf16[1024,128]{1,0:T(8,128)(2,1)S(1)}, bf16[1024,128]{1,0:T(8,128)(2,1)}, u32[]{:S(2)}, u32[]{:S(2)}) collective-permute-start(bf16[1024,128]{1,0:T(8,128)(2,1)S(1)} %bitcast.14), channel_id=1, source_target_pairs={{0,2},{1,3},{2,0},{3,1},{4,6},{5,7},{6,4},{7,5},{8,10},{9,11},{10,... | collective-permute-start | bytes 786440 | tf_op jit(solution)/shard_map/ppermute | solution.py:24
  151.8 17.9 %collective-permute-start.31 = (bf16[1024,128]{1,0:T(8,128)(2,1)S(1)}, bf16[1024,128]{1,0:T(8,128)(2,1)}, u32[]{:S(2)}, u32[]{:S(2)}) collective-permute-start(bf16[1024,128]{1,0:T(8,128)(2,1)S(1)} %bitcast.15), channel_id=1, source_target_pairs={{0,3},{1,0},{2,1},{3,2},{4,7},{5,4},{6,5},{7,6},{8,11},{9,8},{10,9... | collective-permute-start | bytes 786440 | tf_op jit(solution)/shard_map/ppermute | solution.py:24
  152.3 17.3 %collective-permute-start.30 = (bf16[1024,128]{1,0:T(8,128)(2,1)S(1)}, bf16[1024,128]{1,0:T(8,128)(2,1)}, u32[]{:S(2)}, u32[]{:S(2)}) collective-permute-start(bf16[1024,128]{1,0:T(8,128)(2,1)S(1)} %bitcast.16), channel_id=1, source_target_pairs={{0,1},{1,2},{2,3},{3,0},{4,5},{5,6},{6,7},{7,4},{8,9},{9,10},{10,1... | collective-permute-start | bytes 786440 | tf_op jit(solution)/shard_map/ppermute | solution.py:24
  (30 other events, 445.7 us)
